TPU v7x, 32 devices: a whole 2x2x4 slice. The times are simulated.
32 devices in a mesh: pipe: 2 (over core), ctx: 16 (over z, y, x).
Axes of the slice: x: 2, y: 2, z: 4, core: 2. Of those that a mesh axis runs over, the one named last changes fastest.
Arguments:
- states: bfloat16 [2, 2048, 2048], P('pipe', 'ctx'), may hold values from -6 to 6
- norm_gain: float32 [2, 2048], P('pipe'), may hold values from 0.25 to 1.75
- w_in: bfloat16 [2, 2048, 1536], P('pipe', 'ctx'), may hold values from -1 to 1
- w_out: bfloat16 [2, 1024, 2048], P('pipe', 'ctx'), may hold values from -0.1875 to 0.1875
- lengths: int32 [2, 4], replicated, may hold values from 1 to 1024, 2048 in all within a row
Outputs:
- moved: bfloat16 [2, 2048, 2048], P('pipe', 'ctx')
Inputs may be any that keep to these rules, and one draw needn't show every extreme that they name: Each row of lengths lays the responses of one micro-batch end to end over the 2048 positions.
All inputs are finite; a program needn't handle non-finite values.
Results may differ from a plain program's by a relative error of at most 0.0045.
Values may be sent and summed in bfloat16 or wider, within the bound.
No kernel may reach another device: no remote copies, remote signals or barrier semaphores. Data moves between devices by JAX's collectives and lax.ppermute only.
A program may use at most 64 MiB of HBM per device.

v0:
```python
import jax
import jax.numpy as jnp
from jax import lax
from jax.sharding import PartitionSpec as P

HEAD_DIM = 64
HEADS = 16
KV_HEADS = 4


epsilon = 1e-05
rope_base = 500000.0
masked_score = -1e30


def passed_along(value, axis, steps):
    count = lax.axis_size(axis)
    initial, last = (max(0, -steps), min(count, count - steps))
    return lax.ppermute(value, axis, [(source, source + steps) for source in range(initial, last)])


def passed_along_2(value, axis, steps):
    count = lax.axis_size(axis)
    pairs = [(source, (source + steps) % count) for source in range(count)]
    return lax.ppermute(value, axis, pairs)


def locate(doc_lengths, spots):
    doc_ends = jnp.cumsum(doc_lengths)
    segment = jnp.sum((doc_ends[None, :] <= spots[:, None]).astype(jnp.int32), axis=1)
    starts = doc_ends - doc_lengths
    labels = jnp.arange(doc_lengths.shape[0], dtype=jnp.int32)
    first = jnp.sum(jnp.where(segment[:, None] == labels[None, :], starts[None, :], 0), axis=1)
    return (segment, spots - first)


def rotate_pairs(heads_data, position):
    half_dim = heads_data.shape[-1] // 2
    inverse = rope_base ** (-jnp.arange(half_dim, dtype=jnp.float32) * 2.0 / heads_data.shape[-1])
    angles = position.astype(jnp.float32)[:, None] * inverse[None, :]
    cosine = jnp.cos(angles)[:, None, :]
    sine_part = jnp.sin(angles)[:, None, :]
    first_half = heads_data[..., :half_dim]
    second_half = heads_data[..., half_dim:]
    return jnp.concatenate(
        [
            first_half * cosine - second_half * sine_part,
            second_half * cosine + first_half * sine_part,
        ],
        -1,
    )


def body(states, norm_gain, w_in, w_out, lengths):
    section_index = lax.axis_index("pipe")
    ctx_index = lax.axis_index("ctx")
    ctx_count = lax.axis_size("ctx")
    tok_rows = states.shape[1]
    doc_lengths = lax.dynamic_index_in_dim(lengths, section_index, 0, keepdims=False)
    gain = norm_gain[0]
    weight_in = w_in[0]
    weight_out = w_out[0]
    wide = states[0].astype(jnp.float32)
    normed = (wide * lax.rsqrt(jnp.mean(wide * wide, -1, keepdims=True) + epsilon) * gain).astype(
        jnp.bfloat16
    )
    columns = normed
    proj = jnp.dot(
        columns,
        lax.all_gather(weight_in, "ctx", axis=0, tiled=True),
        preferred_element_type=jnp.float32,
    )
    q_width = HEADS * HEAD_DIM
    k_width = KV_HEADS * HEAD_DIM
    group = HEADS // KV_HEADS
    first_spot = ctx_index * tok_rows
    query_spots = first_spot + jnp.arange(tok_rows, dtype=jnp.int32)
    query_seg, position = locate(doc_lengths, query_spots)
    queries = rotate_pairs(proj[:, :q_width].reshape(tok_rows, HEADS, HEAD_DIM), position).astype(
        jnp.bfloat16
    )
    queries = queries.reshape(tok_rows, KV_HEADS, group, HEAD_DIM)
    keys_rot = rotate_pairs(
        proj[:, q_width : q_width + k_width].reshape(tok_rows, KV_HEADS, HEAD_DIM), position
    ).astype(jnp.bfloat16)
    values = proj[:, q_width + k_width :].astype(jnp.bfloat16)
    key_values = jnp.concatenate([keys_rot.reshape(tok_rows, k_width), values], 1)

    def attend_block(carry, portion, offset):
        row_count = portion.shape[0]
        key_spots = offset + jnp.arange(row_count, dtype=jnp.int32)
        key_seg, unused_place = locate(doc_lengths, key_spots)
        allowed = (
            (query_seg[:, None] == key_seg[None, :])
            & (key_spots[None, :] <= query_spots[:, None])
            & (key_spots[None, :] >= 0)
        )

        def update(state):
            running_max, running_sum, accum = state
            key_part = portion[:, :k_width].reshape(row_count, KV_HEADS, HEAD_DIM)
            value_part = portion[:, k_width:].reshape(row_count, KV_HEADS, HEAD_DIM)
            scores = jnp.einsum(
                "tgjd,rgd->gjtr", queries, key_part, preferred_element_type=jnp.float32
            ) * HEAD_DIM ** (-0.5)
            scores = jnp.where(allowed, scores, masked_score)
            new_max = jnp.maximum(running_max, jnp.max(scores, -1))
            rescale = jnp.exp(running_max - new_max)
            probs = jnp.where(allowed, jnp.exp(scores - new_max[..., None]), 0.0)
            new_sum = running_sum * rescale + jnp.sum(probs, -1)
            product = jnp.einsum(
                "gjtr,rgd->gjtd",
                probs.astype(jnp.bfloat16),
                value_part,
                preferred_element_type=jnp.float32,
            )
            return (new_max, new_sum, accum * rescale[..., None] + product)

        return lax.cond(jnp.any(allowed), update, lambda state: state, carry)

    initial = (
        jnp.full((KV_HEADS, group, tok_rows), masked_score, jnp.float32),
        jnp.zeros((KV_HEADS, group, tok_rows), jnp.float32),
        jnp.zeros((KV_HEADS, group, tok_rows, HEAD_DIM), jnp.float32),
    )
    resp_longest = min(1024, 8 * tok_rows, tok_rows * ctx_count // 2)
    reach_count = min(ctx_count - 1, (resp_longest + tok_rows - 2) // tok_rows)
    needed = reach_count + 1
    collected = key_values
    held = 1
    while held < needed:
        taken = min(held, needed - held)
        arrived = passed_along(collected[collected.shape[0] - taken * tok_rows :], "ctx", held)
        collected = jnp.concatenate([arrived, collected], 0)
        held = held + taken
    carry = initial
    portion = collected
    offset = first_spot - (held - 1) * tok_rows
    row_count = portion.shape[0]
    block_rows = min(row_count, 512)
    full_blocks = row_count // block_rows

    def visit_block(block_idx, state):
        sliced = lax.dynamic_slice_in_dim(portion, block_idx * block_rows, block_rows, 0)
        return attend_block(state, sliced, offset + block_idx * block_rows)

    carry = lax.fori_loop(0, full_blocks, visit_block, carry)
    carry = attend_block(
        carry, portion[full_blocks * block_rows :], offset + full_blocks * block_rows
    )
    running_max, running_sum, accum = carry
    attended = (
        (accum / running_sum[..., None])
        .transpose(2, 0, 1, 3)
        .reshape(tok_rows, q_width)
        .astype(jnp.bfloat16)
    )
    columns = attended
    output = jnp.dot(
        columns,
        lax.all_gather(weight_out, "ctx", axis=0, tiled=True),
        preferred_element_type=jnp.float32,
    )
    new_state = (wide + output).astype(jnp.bfloat16)
    passed = passed_along_2(new_state, "pipe", 1)
    return passed[None]


def solution(mesh):
    return jax.shard_map(
        body,
        mesh=mesh,
        in_specs=(
            P("pipe", "ctx", None),
            P("pipe", None),
            P("pipe", "ctx", None),
            P("pipe", "ctx", None),
            P(),
        ),
        out_specs=P("pipe", "ctx", None),
        check_vma=False,
    )
```

profile of v0, /device:TPU:17, one launch (start us, length us, event | category | flops | bytes accessed | tf_op | source)
XLA Modules:
  0.0 201.4 jit_solution(16966979567751797768)
XLA Ops:
  6.5 0.0 all-gather.5.cloned.1.call-start
  6.5 0.7 all-gather.5.cloned.1.call-update
  7.3 0.0 all-gather.7.cloned.1.call-start
  7.3 0.7 all-gather.7.cloned.1.call-update
  8.0 0.7 fusion.52
  8.7 0.2 reduce-window.6
  8.9 0.1 convert_reduce_fusion.1
  9.0 0.7 fusion.41
  9.7 0.1 select_reduce_fusion
  9.8 1.2 fusion.34
  11.0 0.1 multiply_cosine_fusion
  11.1 91.9 %all-gather.5.cloned.1.call-done = bf16[1,2048,1536]{2,1,0:T(8,128)(2,1)} async-done(((bf16[1,128,1536]{2,1,0:T(8,128)(2,1)}), bf16[1,2048,1536]{2,1,0:T(8,128)(2,1)}) %all-gather.5.cloned.1.call-update) | async-done | bytes 6291472 | tf_op jit(solution)/shard_map/all_gather | solution.py:70
  103.0 0.0 copy-start.2
  103.0 4.0 %fusion.24 = f32[128,1536]{1,0:T(8,128)S(1)} fusion(bf16[1,2048,1536]{2,1,0:T(8,128)(2,1)} %all-gather.5.cloned.1.call-done, bf16[1,128,2048]{2,1,0:T(8,128)(2,1)} %param.11, f32[2048]{0:T(1024)} %bitcast.120, f32[128]{0:T(128)S(1)} %add_rsqrt_fusion), kind=kOutput, calls=%fused_computation.34 | convolution fusion | flops 806354944 | bytes 7610880 | tf_op jit(solution)/shard_map/dot_general | solution.py:68
  107.1 0.1 copy.26
  107.2 0.1 copy.27
  107.4 0.7 pad_maximum_fusion.1
  108.0 3.1 %collective-permute-start.1 = (bf16[128,512]{1,0:T(8,128)(2,1)}, bf16[128,512]{1,0:T(8,128)(2,1)S(1)}, u32[]{:S(2)}, u32[]{:S(2)}) collective-permute-start(bf16[128,512]{1,0:T(8,128)(2,1)} %pad_maximum_fusion.1), channel_id=1, source_target_pairs={{0,1},{1,2},{2,3},{3,4},{4,5},{5,6},{6,7},{7,8},{8,9},{9,10},{10,1... | collective-permute-start | bytes 393224 | tf_op jit(solution)/shard_map/ppermute | solution.py:19
  111.1 4.6 %collective-permute-done.1 = bf16[128,512]{1,0:T(8,128)(2,1)S(1)} collective-permute-done((bf16[128,512]{1,0:T(8,128)(2,1)}, bf16[128,512]{1,0:T(8,128)(2,1)S(1)}, u32[]{:S(2)}, u32[]{:S(2)}) %collective-permute-start.1) | collective-permute-done | bytes 131104 | tf_op jit(solution)/shard_map/ppermute | solution.py:19
  115.8 2.2 %collective-permute-start.2 = (bf16[256,512]{1,0:T(8,128)(2,1)S(1)}, bf16[256,512]{1,0:T(8,128)(2,1)S(1)}, u32[]{:S(2)}, u32[]{:S(2)}) collective-permute-start(bf16[256,512]{1,0:T(8,128)(2,1)S(1)} %maximum_maximum_fusion.1), channel_id=1, source_target_pairs={{0,2},{1,3},{2,4},{3,5},{4,6},{5,7},{6,8},{7,9},{8,10},{9,11},{10,... | collective-permute-start | bytes 786440 | tf_op jit(solution)/shard_map/ppermute | solution.py:19
  118.0 1.4 and_and_fusion.1
  119.4 9.7 %collective-permute-done.2 = bf16[256,512]{1,0:T(8,128)(2,1)S(1)} collective-permute-done((bf16[256,512]{1,0:T(8,128)(2,1)S(1)}, bf16[256,512]{1,0:T(8,128)(2,1)S(1)}, u32[]{:S(2)}, u32[]{:S(2)}) %collective-permute-start.2) | collective-permute-done | bytes 262176 | tf_op jit(solution)/shard_map/ppermute | solution.py:19
  129.1 3.8 %collective-permute-start.3 = (bf16[512,512]{1,0:T(8,128)(2,1)S(1)}, bf16[512,512]{1,0:T(8,128)(2,1)S(1)}, u32[]{:S(2)}, u32[]{:S(2)}) collective-permute-start(bf16[512,512]{1,0:T(8,128)(2,1)S(1)} %maximum_maximum_fusion), channel_id=1, source_target_pairs={{0,4},{1,5},{2,6},{3,7},{4,8},{5,9},{6,10},{7,11},{8,12},{9,13},{1... | collective-permute-start | bytes 1572872 | tf_op jit(solution)/shard_map/ppermute | solution.py:19
  132.9 0.0 copy-done.2
  132.9 0.2 broadcast_in_dim.105
  133.8 1.3 collective-permute-start
  135.2 0.2 copy.28
  135.4 0.1 subtract_convert_fusion
  135.5 18.7 %collective-permute-done = bf16[128,512]{1,0:T(8,128)(2,1)} collective-permute-done((bf16[128,512]{1,0:T(8,128)(2,1)}, bf16[128,512]{1,0:T(8,128)(2,1)}, u32[]{:S(2)}, u32[]{:S(2)}) %collective-permute-start) | collective-permute-done | bytes 131104 | tf_op jit(solution)/shard_map/ppermute | solution.py:19
  154.2 1.5 constant_dynamic-update-slice_fusion.4
  155.7 0.8 collective-permute-done.3
  156.5 0.8 constant_dynamic-update-slice_fusion.3
  157.4 0.7 constant_dynamic-update-slice_fusion.2
  158.1 0.7 constant_dynamic-update-slice_fusion.1
  158.7 0.7 constant_dynamic-update-slice_fusion
  159.4 1.7 copy.29
  161.1 0.0 copy-start.1
  161.2 3.7 %while.20 = (s32[]{:T(128)}, f32[4,4,128]{2,1,0:T(4,128)S(1)}, f32[4,4,128]{2,1,0:T(4,128)S(1)}, f32[4,4,128,64]{2,3,1,0:T(8,128)S(1)}, s32[128]{0:T(128)S(1)}, ...) while((s32[]{:T(128)}, f32[4,4,128]{2,1,0:T(4,128)S(1)}, ...), condition=%wide.region_13.14_spmd.clone, body=%wide.region_6.13_spmd.clone.sunk | while | flops 282668160 | bytes 15872853 | solution.py:147
  161.2 0.1 convert_reduce_fusion.3
  161.3 1.0 fusion.54
  163.0 0.1 convert_reduce_fusion.3
  163.1 1.0 fusion.54
  164.8 0.0 copy-start
  164.8 0.0 copy-done.1
  164.9 1.1 conditional.2
  164.9 0.4 fusion.45
  165.3 0.2 fusion.17
  165.5 0.1 copy.30
  165.6 0.4 convolution_add_fusion
  166.0 0.1 divide_convert_fusion
  166.0 21.8 %all-gather.7.cloned.1.call-done = bf16[1,1024,2048]{2,1,0:T(8,128)(2,1)} async-done(((bf16[1,64,2048]{2,1,0:T(8,128)(2,1)}), bf16[1,1024,2048]{2,1,0:T(8,128)(2,1)}) %all-gather.7.cloned.1.call-update) | async-done | bytes 4194320 | tf_op jit(solution)/shard_map/all_gather | solution.py:161
  187.8 0.0 copy-done
  187.8 2.9 %fusion.31 = bf16[128,2048]{1,0:T(8,128)(2,1)S(1)} fusion(bf16[128,1024]{0,1:T(8,128)(2,1)S(1)} %bitcast.103, bf16[1,1024,2048]{2,1,0:T(8,128)(2,1)} %all-gather.7.cloned.1.call-done, bf16[1,128,2048]{2,1,0:T(8,128)(2,1)S(1)} %copy-done), kind=kOutput, calls=%fused_computation.39 | convolution fusion | flops 537657344 | bytes 5505024 | tf_op jit(solution)/shard_map/dot_general | solution.py:159
  190.7 1.5 collective-permute-start.4
  192.2 1.5 collective-permute-done.4
  193.7 0.8 copy.66
  (27 shorter events, 0.3 us)
Async XLA Ops:
  6.5 96.5 %all-gather.5.cloned.1.call-start = ((), (), s32[]{:S(2)}) async-start(), calls=%async_computation | async-start | bytes 6684672 | tf_op jit(solution)/shard_map/all_gather | solution.py:70
  7.3 180.5 %all-gather.7.cloned.1.call-start = ((), (), s32[]{:S(2)}) async-start(), calls=%async_computation.1 | async-start | bytes 4456448 | tf_op jit(solution)/shard_map/all_gather | solution.py:161
  103.0 29.9 %copy-start.2 = (s32[2,4]{1,0:T(2,128)S(1)}, s32[2,4]{1,0:T(2,128)}, u32[]{:S(2)}) copy-start(s32[2,4]{1,0:T(2,128)} %param.15) | copy-start | bytes 100
  108.0 7.7 %collective-permute-start.1 = (bf16[128,512]{1,0:T(8,128)(2,1)}, bf16[128,512]{1,0:T(8,128)(2,1)S(1)}, u32[]{:S(2)}, u32[]{:S(2)}) collective-permute-start(bf16[128,512]{1,0:T(8,128)(2,1)} %pad_maximum_fusion.1), channel_id=1, source_target_pairs={{0,1},{1,2},{2,3},{3,4},{4,5},{5,6},{6,7},{7,8},{8,9},{9,10},{10,1... | collective-permute-start | bytes 393224 | tf_op jit(solution)/shard_map/ppermute | solution.py:19
  115.8 13.3 %collective-permute-start.2 = (bf16[256,512]{1,0:T(8,128)(2,1)S(1)}, bf16[256,512]{1,0:T(8,128)(2,1)S(1)}, u32[]{:S(2)}, u32[]{:S(2)}) collective-permute-start(bf16[256,512]{1,0:T(8,128)(2,1)S(1)} %maximum_maximum_fusion.1), channel_id=1, source_target_pairs={{0,2},{1,3},{2,4},{3,5},{4,6},{5,7},{6,8},{7,9},{8,10},{9,11},{10,... | collective-permute-start | bytes 786440 | tf_op jit(solution)/shard_map/ppermute | solution.py:19
  129.1 27.4 %collective-permute-start.3 = (bf16[512,512]{1,0:T(8,128)(2,1)S(1)}, bf16[512,512]{1,0:T(8,128)(2,1)S(1)}, u32[]{:S(2)}, u32[]{:S(2)}) collective-permute-start(bf16[512,512]{1,0:T(8,128)(2,1)S(1)} %maximum_maximum_fusion), channel_id=1, source_target_pairs={{0,4},{1,5},{2,6},{3,7},{4,8},{5,9},{6,10},{7,11},{8,12},{9,13},{1... | collective-permute-start | bytes 1572872 | tf_op jit(solution)/shard_map/ppermute | solution.py:19
  133.8 20.3 %collective-permute-start = (bf16[128,512]{1,0:T(8,128)(2,1)}, bf16[128,512]{1,0:T(8,128)(2,1)}, u32[]{:S(2)}, u32[]{:S(2)}) collective-permute-start(bf16[128,512]{1,0:T(8,128)(2,1)} %pad_maximum_fusion.1), channel_id=1, source_target_pairs={{0,8},{1,9},{2,10},{3,11},{4,12},{5,13},{6,14},{7,15},{16,24},{17,... | collective-permute-start | bytes 393224 | tf_op jit(solution)/shard_map/ppermute | solution.py:19
  161.1 3.7 %copy-start.1 = (pred[128,128]{0,1:T(8,128)(4,1)S(1)}, pred[128,128]{0,1:T(8,128)(4,1)}, u32[]{:S(2)}) copy-start(pred[128,128]{0,1:T(8,128)(4,1)} %get-tuple-element.457) | copy-start | bytes 49156
  164.8 23.0 %copy-start = (bf16[1,128,2048]{2,1,0:T(8,128)(2,1)S(1)}, bf16[1,128,2048]{2,1,0:T(8,128)(2,1)}, u32[]{:S(2)}) copy-start(bf16[1,128,2048]{2,1,0:T(8,128)(2,1)} %param.11) | copy-start | bytes 1572868
  190.7 3.0 %collective-permute-start.4 = (bf16[128,2048]{1,0:T(8,128)(2,1)S(1)}, bf16[128,2048]{1,0:T(8,128)(2,1)S(1)}, u32[]{:S(2)}, u32[]{:S(2)}) collective-permute-start(bf16[128,2048]{1,0:T(8,128)(2,1)S(1)} %fusion.31), channel_id=1, source_target_pairs={{0,16},{16,0},{1,17},{17,1},{2,18},{18,2},{3,19},{19,3},{4,20},{20... | collective-permute-start | bytes 1572872 | tf_op jit(solution)/shard_map/ppermute | solution.py:25
Sparse Core Ops, SparseCore 0:
  10.1 92.8 all-gather.4
  105.8 81.9 all-gather.6
where the time goes:
time: 204 us; the launch traced here: 201 us
  waiting for transfers between devices  150 us (74%)
  between operations  14.4 us (7%)
  starting transfers between devices  11.8 us (6%)
  other arithmetic  7.99 us (4%)
  matrix products  7.68 us (4%)
  local copies, waits for them, and re-layouts  7.54 us (4%)
    all_gather x1, waiting for transfers between devices, body(): lax.all_gather(weight_in, 'ctx', axis=0, tiled=True)  91.9 us
    ppermute x4, waiting for transfers between devices, passed_along(): lax.ppermute(value, axis, [(source, source + steps) for source in range(i...  33.8 us
    all_gather x1, waiting for transfers between devices, body(): lax.all_gather(weight_out, 'ctx', axis=0, tiled=True)  21.8 us
    ppermute x4, starting transfers between devices, passed_along(): lax.ppermute(value, axis, [(source, source + steps) for source in range(i...  10.3 us
    unnamed x12, local copies, waits for them, and re-layouts  6.24 us
  transfers between devices with their start and end apart: 7, of which 7 were waited for; matrix products, arithmetic and copies ran while one was open for 10% of the time, Pallas kernels for 0%

commit v1 on v0

v1 whole, which is shorter than its diff:
```python
import functools

import jax
import jax.numpy as jnp
from jax import lax
from jax.experimental import pallas as pl
from jax.experimental.pallas import tpu as pltpu
from jax.sharding import PartitionSpec as P

HEAD_DIM = 64
HEADS = 16
KV_HEADS = 4
GROUP = HEADS // KV_HEADS

epsilon = 1e-05
rope_base = 500000.0
masked_score = -1e30
KEY_BLOCK = 256

VMEM = pltpu.MemorySpace.VMEM
SMEM = pltpu.MemorySpace.SMEM


def call(kernel, out_shape, scratch=(), flops=0, moved=0):
    def run(scalars, *arrays):
        return pl.pallas_call(
            kernel,
            out_shape=out_shape,
            in_specs=[pl.BlockSpec(memory_space=SMEM)]
            + [pl.BlockSpec(memory_space=VMEM)] * len(arrays),
            out_specs=jax.tree.map(lambda _: pl.BlockSpec(memory_space=VMEM), out_shape),
            scratch_shapes=list(scratch),
            cost_estimate=pl.CostEstimate(flops=flops, bytes_accessed=moved, transcendentals=0),
        )(scalars, *arrays)

    return run


def stack_kernel(s_ref, b0, b1, b2, b3, out_ref):
    size = b0.shape[0]
    for k, ref in enumerate((b0, b1, b2, b3)):
        at = pl.multiple_of(lax.bitwise_xor(s_ref[1], k) * size, 16)
        out_ref[pl.ds(at, size), :] = ref[...]


def norm_kernel(s_ref, x0, x1, x2, x3a, x3b, gain_ref, normed_ref, rest_ref):
    col = s_ref[1]
    rows = x0.shape[0]
    tile = rest_ref.shape[1]

    def one(ref, first, count, place):
        wide = ref[...].astype(jnp.float32)
        scale = lax.rsqrt(jnp.mean(wide * wide, -1, keepdims=True) + epsilon)
        at = pl.ds(pl.multiple_of(place * rows + first, 8), count)
        normed_ref[at, :] = (wide * scale * gain_ref[...]).astype(jnp.bfloat16)
        rest_ref[at, :] = ref[:, pl.ds(pl.multiple_of(col * tile, 128), tile)]

    half = rows // 2
    one(x0, 0, rows, col)
    one(x1, 0, rows, lax.bitwise_xor(col, 1))
    one(x2, 0, rows, lax.bitwise_xor(col, 2))
    one(x3a, 0, half, lax.bitwise_xor(col, 3))
    one(x3b, half, half, lax.bitwise_xor(col, 3))


def rotated(part, cosine, sine):
    lane = lax.broadcasted_iota(jnp.int32, part.shape, 1)
    half = HEAD_DIM // 2
    ahead = pltpu.roll(part, 128 - half, 1)
    behind = pltpu.roll(part, half, 1)
    other = jnp.where(lax.rem(lane, HEAD_DIM) < half, ahead, behind)
    return part * cosine + other * sine


def qkv_kernel(count, s_ref, normed_ref, cos_ref, sin_ref, *refs):
    blocks, (q_ref, kv_ref) = refs[:count], refs[count:]
    deep = blocks[0].shape[0]
    proj = None
    for d in range(count):
        cols = pl.ds(pl.multiple_of(s_ref[8 + d] * deep, 128), deep)
        term = jnp.dot(normed_ref[:, cols], blocks[d][...], preferred_element_type=jnp.float32)
        proj = term if proj is None else proj + term
    cosine, sine = cos_ref[...], sin_ref[...]
    wide = GROUP * HEAD_DIM
    for g in range(wide // 128):
        part = rotated(proj[:, g * 128 : (g + 1) * 128], cosine, sine)
        q_ref[:, g * 128 : (g + 1) * 128] = (part * HEAD_DIM ** (-0.5)).astype(jnp.bfloat16)
    part = proj[:, wide : wide + 128]
    lane = lax.broadcasted_iota(jnp.int32, part.shape, 1)
    kv_ref[...] = jnp.where(lane < HEAD_DIM, rotated(part, cosine, sine), part).astype(jnp.bfloat16)


def attention_kernel(docs, reach, s_ref, q_ref, *refs):
    kv_refs = refs[: reach + 1]
    out_ref, kv_all, scores, top, total, accum = refs[reach + 1 :]
    span, tile = q_ref.shape[0], 128
    base = (s_ref[0] - reach) * span
    for r in range(reach + 1):
        kv_all[r * span : (r + 1) * span, :] = kv_refs[r][...]

    def doc_start(spots):
        ends, start = 0, spots * 0
        for d in range(docs):
            long = s_ref[32 + d]
            ends = ends + long
            start = start + jnp.where(spots >= ends, long, 0)
        return start

    @pl.loop(0, span // tile)
    def _(i):
        first = s_ref[0] * span + i * tile
        rows = pl.ds(pl.multiple_of(i * tile, tile), tile)
        low = lax.max(doc_start(first) - base, 0) // KEY_BLOCK
        high = (first + tile - 1 - base) // KEY_BLOCK + 1
        flat = q_ref[rows, :]
        blank = jnp.zeros((tile, 128 - HEAD_DIM), jnp.bfloat16)
        stacked = jnp.concatenate(
            [
                jnp.concatenate([flat[:, h * HEAD_DIM : (h + 1) * HEAD_DIM], blank], 1)
                for h in range(GROUP)
            ],
            0,
        )
        spots = first + lax.broadcasted_iota(jnp.int32, (tile, 1), 0)
        starts = doc_start(spots)
        top[...] = jnp.full(top.shape, masked_score, jnp.float32)

        @pl.loop(low, high)
        def _(j):
            keys = kv_all[pl.ds(pl.multiple_of(j * KEY_BLOCK, KEY_BLOCK), KEY_BLOCK), :]
            part = lax.dot_general(
                stacked, keys, (((1,), (1,)), ((), ())), preferred_element_type=jnp.float32
            )
            key_spots = (
                base + j * KEY_BLOCK + lax.broadcasted_iota(jnp.int32, (tile, KEY_BLOCK), 1)
            )
            allowed = (key_spots <= spots) & (key_spots >= starts)
            for h in range(GROUP):
                at = slice(h * tile, (h + 1) * tile)
                kept = jnp.where(allowed, part[at], masked_score)
                scores[j, at, :] = kept
                best = top[at, :]
                for k in range(KEY_BLOCK // 128):
                    best = jnp.maximum(best, kept[:, k * 128 : (k + 1) * 128])
                top[at, :] = best

        highest = jnp.max(top[...], -1, keepdims=True)
        total[...] = jnp.zeros(total.shape, jnp.float32)
        accum[...] = jnp.zeros(accum.shape, jnp.float32)

        @pl.loop(low, high)
        def _(j):
            probs = jnp.exp(scores[j] - highest)
            added = total[...]
            for k in range(KEY_BLOCK // 128):
                added = added + probs[:, k * 128 : (k + 1) * 128]
            total[...] = added
            both = kv_all[pl.ds(pl.multiple_of(j * KEY_BLOCK, KEY_BLOCK), KEY_BLOCK), :]
            accum[...] += jnp.dot(
                probs.astype(jnp.bfloat16), both, preferred_element_type=jnp.float32
            )

        done = accum[...] / jnp.sum(total[...], -1, keepdims=True)
        out_ref[rows, :] = jnp.concatenate(
            [done[h * tile : (h + 1) * tile, HEAD_DIM : 2 * HEAD_DIM] for h in range(GROUP)], 1
        ).astype(jnp.bfloat16)


def output_kernel(count, s_ref, a0, a1, a2, a3a, a3b, rest_ref, *refs):
    blocks = refs[:count]
    outs = refs[count : count + KV_HEADS]
    weight = refs[count + KV_HEADS]
    col = s_ref[1]
    deep = blocks[0].shape[0]
    span, each = a0.shape
    for d in range(count):
        row = pl.multiple_of(s_ref[8 + d] * deep, 128)
        weight[pl.ds(row, deep), :] = blocks[d][...]

    def rows_of(k):
        place = lax.bitwise_xor(col, k) * each
        return weight[pl.ds(pl.multiple_of(place, 128), each), :]

    w0, w1, w2, w3 = rows_of(0), rows_of(1), rows_of(2), rows_of(3)
    size = span // KV_HEADS
    for k in range(KV_HEADS):
        token = lax.bitwise_xor(col, k)
        at = pl.ds(pl.multiple_of(token * size, size), size)
        later = token >= KV_HEADS // 2
        there = pl.ds(pl.multiple_of(lax.rem(token, KV_HEADS // 2) * size, size), size)
        third = jnp.where(later, a3b[there, :], a3a[there, :])
        value = jnp.dot(a0[at, :], w0, preferred_element_type=jnp.float32)
        value += jnp.dot(a1[at, :], w1, preferred_element_type=jnp.float32)
        value += jnp.dot(a2[at, :], w2, preferred_element_type=jnp.float32)
        value += jnp.dot(third, w3, preferred_element_type=jnp.float32)
        outs[k][...] = (rest_ref[at, :].astype(jnp.float32) + value).astype(jnp.bfloat16)


def place_kernel(s_ref, r0, r1, r2, r3, out_ref):
    width = r0.shape[1]
    for k, ref in enumerate((r0, r1, r2, r3)):
        at = pl.multiple_of(lax.bitwise_xor(s_ref[1], k) * width, 128)
        out_ref[:, pl.ds(at, width)] = ref[...]


def doc_starts(doc_lengths, spots):
    ends = jnp.cumsum(doc_lengths)
    return jnp.sum(jnp.where(ends[None, :] <= spots[:, None], doc_lengths[None, :], 0), axis=1)


def body(states, norm_gain, w_in, w_out, lengths):
    section = lax.axis_index("pipe")
    sections = lax.axis_size("pipe")
    me = lax.axis_index("ctx")
    count = lax.axis_size("ctx")
    planes = count // KV_HEADS
    col = lax.rem(me, KV_HEADS)
    plane = me // KV_HEADS
    x = states[0]
    rows, width = x.shape
    span = rows * KV_HEADS
    tile = width // KV_HEADS
    q_width, k_width = HEADS * HEAD_DIM, KV_HEADS * HEAD_DIM
    each = GROUP * HEAD_DIM

    order = list(range(0, planes, 2)) + list(range(1, planes, 2))[::-1]
    ring = [
        (order[i] * KV_HEADS + c, order[(i + 1) % planes] * KV_HEADS + c)
        for i in range(planes)
        for c in range(KV_HEADS)
    ]

    def across(value, k):
        return lax.ppermute(value, "ctx", [(i, i ^ k) for i in range(count)])

    def exchanged(blocks):
        own = lax.dynamic_index_in_dim(blocks, col, 0, keepdims=False)
        got = [
            across(lax.dynamic_index_in_dim(blocks, lax.bitwise_xor(col, k), 0, keepdims=False), k)
            for k in range(1, KV_HEADS)
        ]
        size, wide = own.shape
        shape = jax.ShapeDtypeStruct((KV_HEADS * size, wide), own.dtype)
        return call(stack_kernel, shape, moved=4 * KV_HEADS * size * wide)(scalars, own, *got)

    def ringed(block):
        held = [block]
        for _ in range(planes - 1):
            held.append(lax.ppermute(held[-1], "ctx", ring))
        return held

    def gathered(value):
        half = value.shape[0] // 2
        one, two = across(value, 1), across(value, 2)
        return [value, one, two, across(one[:half], 2), across(two[half:], 1)]

    doc_lengths = lax.dynamic_index_in_dim(lengths, section, 0, keepdims=False)
    docs = doc_lengths.shape[0]
    place_in_ring = jnp.zeros((), jnp.int32)
    for i, p in enumerate(order):
        place_in_ring = jnp.where(plane == p, i, place_in_ring)
    steps = lax.rem(place_in_ring - jnp.arange(planes, dtype=jnp.int32) + planes, planes)
    holders = jnp.where(2 * steps < planes + planes % 2, 2 * steps, 2 * (planes - 1 - steps) + 1)
    scalars = jnp.zeros((64,), jnp.int32)
    scalars = scalars.at[0].set(plane).at[1].set(col)
    scalars = scalars.at[8 : 8 + planes].set(holders).at[32 : 32 + docs].set(doc_lengths)

    w = w_in[0]
    by_col = jnp.concatenate(
        [
            w[:, :q_width].reshape(-1, KV_HEADS, each),
            w[:, q_width : q_width + k_width].reshape(-1, KV_HEADS, HEAD_DIM),
            w[:, q_width + k_width :].reshape(-1, KV_HEADS, HEAD_DIM),
        ],
        2,
    ).transpose(1, 0, 2)
    in_blocks = ringed(exchanged(by_col))
    out_by_col = w_out[0].reshape(-1, KV_HEADS, tile).transpose(1, 0, 2)

    parts = gathered(x)
    normed, rest = call(
        norm_kernel,
        (
            jax.ShapeDtypeStruct((span, width), jnp.bfloat16),
            jax.ShapeDtypeStruct((span, tile), jnp.bfloat16),
        ),
        moved=4 * span * width,
    )(scalars, *parts, norm_gain)

    spots = plane * span + jnp.arange(span, dtype=jnp.int32)
    position = (spots - doc_starts(doc_lengths, spots)).astype(jnp.float32)
    half = HEAD_DIM // 2
    inverse = rope_base ** (-jnp.arange(half, dtype=jnp.float32) * 2.0 / HEAD_DIM)
    angles = position[:, None] * inverse[None, :]
    cosine = jnp.tile(jnp.cos(angles), (1, 128 // half))
    sine = jnp.sin(angles)
    sine = jnp.tile(jnp.concatenate([-sine, sine], 1), (1, 128 // HEAD_DIM))

    queries, keys_values = call(
        functools.partial(qkv_kernel, planes),
        (
            jax.ShapeDtypeStruct((span, each), jnp.bfloat16),
            jax.ShapeDtypeStruct((span, 2 * HEAD_DIM), jnp.bfloat16),
        ),
        flops=2 * span * width * (each + 2 * HEAD_DIM),
        moved=2 * span * width + 2 * width * (each + 2 * HEAD_DIM),
    )(scalars, normed, cosine, sine, *in_blocks)

    longest = min(1024, 8 * rows, rows * count // 2)
    reach = min(planes - 1, (longest + span - 2) // span)
    history = [keys_values]
    for r in range(1, reach + 1):
        pairs = [(i, i + r * KV_HEADS) for i in range(count - r * KV_HEADS)]
        history.insert(0, lax.ppermute(keys_values, "ctx", pairs))

    out_blocks = ringed(exchanged(out_by_col))

    key_blocks = (reach + 1) * span // KEY_BLOCK
    attended = call(
        functools.partial(attention_kernel, docs, reach),
        jax.ShapeDtypeStruct((span, each), jnp.bfloat16),
        scratch=[
            pltpu.VMEM(((reach + 1) * span, 2 * HEAD_DIM), jnp.bfloat16),
            pltpu.VMEM((key_blocks, GROUP * 128, KEY_BLOCK), jnp.float32),
            pltpu.VMEM((GROUP * 128, 128), jnp.float32),
            pltpu.VMEM((GROUP * 128, 128), jnp.float32),
            pltpu.VMEM((GROUP * 128, 2 * HEAD_DIM), jnp.float32),
        ],
        flops=8 * span * each * span,
        moved=4 * span * each,
    )(scalars, queries, *history)

    results = call(
        functools.partial(output_kernel, planes),
        (jax.ShapeDtypeStruct((rows, tile), jnp.bfloat16),) * KV_HEADS,
        scratch=[pltpu.VMEM((q_width, tile), jnp.bfloat16)],
        flops=2 * span * q_width * tile,
        moved=2 * q_width * tile + 4 * span * tile,
    )(scalars, *gathered(attended), rest, *out_blocks)

    landed = []
    for k in range(KV_HEADS):
        pairs = [
            (s * count + i, (s + 1) % sections * count + (i ^ k))
            for s in range(sections)
            for i in range(count)
        ]
        landed.append(lax.ppermute(results[k], ("pipe", "ctx"), pairs))
    moved = call(place_kernel, jax.ShapeDtypeStruct((rows, width), jnp.bfloat16), moved=4 * rows * width)(
        scalars, *landed
    )
    return moved[None]


def solution(mesh):
    return jax.shard_map(
        body,
        mesh=mesh,
        in_specs=(
            P("pipe", "ctx", None),
            P("pipe", None),
            P("pipe", "ctx", None),
            P("pipe", "ctx", None),
            P(),
        ),
        out_specs=P("pipe", "ctx", None),
        check_vma=False,
    )
```

time: 204 us -> 113 us (0.55); the launches traced: 201 us -> 113 us
  waiting for transfers between devices: 150 us -> 31.3 us
  starting transfers between devices: 11.8 us -> 45.5 us
  Pallas kernels: 0 us -> 23.3 us
  between operations: 14.4 us -> 0.35 us
  matrix products: 7.68 us -> 0 us
  other arithmetic: 7.99 us -> 0.81 us
  local copies, waits for them, and re-layouts: 7.54 us -> 11.9 us
    all_gather x2 -> x0, waiting for transfers between devices: 114 us -> none  [the longest x1 91.9 us: body(): lax.all_gather(weight_in, 'ctx', axis=0, tiled=True)]
    ppermute x5 -> x26, starting transfers between devices: 11.8 us -> 45.5 us  [the longest x4 20.2 us: body(): landed.append(lax.ppermute(results[k], ('pipe', 'ctx'), pairs))]
    pallas_call x0 -> x7, Pallas kernels: none -> 23.3 us  [run(): pl.pallas_call(kernel, out_shape=out_shape, in_specs=[pl.BlockSpec(memory...]
    dot_general x4 -> x0, matrix products: 7.68 us -> none  [the longest x1 4.02 us: body(): jnp.dot(columns, lax.all_gather(weight_in, 'ctx', axis=0, tiled=True), pr...]
    ppermute x5 -> x26, waiting for transfers between devices: 35.4 us -> 31.3 us  [the longest x14 10.6 us: across(): return lax.ppermute(value, 'ctx', [(i, i ^ k) for i in range(count)])]
    another operation x1 -> x7, local copies, waits for them, and re-layouts: 0.11 us -> 2.48 us  [the longest x2 0.87 us: body(): sine = jnp.tile(jnp.concatenate([-sine, sine], 1), (1, 128 // HEAD_DIM))]
    unnamed x12 -> x63, local copies, waits for them, and re-layouts: 6.24 us -> 7.29 us
  transfers between devices with their start and end apart: 7 -> 26, of which waited for: 7 -> 14; matrix products, arithmetic and copies ran while one was open for 10% -> 4% of each run, Pallas kernels for 0% -> 14%
where the time goes in v1:
time: 113 us
  starting transfers between devices  45.5 us (40%)
  waiting for transfers between devices  31.3 us (28%)
  Pallas kernels  23.3 us (21%)
  local copies, waits for them, and re-layouts  11.9 us (11%)
    pallas_call x7, Pallas kernels, run(): pl.pallas_call(kernel, out_shape=out_shape, in_specs=[pl.BlockSpec(memory...  23.3 us
    ppermute x4, starting transfers between devices, body(): landed.append(lax.ppermute(results[k], ('pipe', 'ctx'), pairs))  20.2 us
    ppermute x14, starting transfers between devices, across(): return lax.ppermute(value, 'ctx', [(i, i ^ k) for i in range(count)])  15.2 us
    ppermute x14, waiting for transfers between devices, across(): return lax.ppermute(value, 'ctx', [(i, i ^ k) for i in range(count)])  10.6 us
    ppermute x6, waiting for transfers between devices, ringed(): held.append(lax.ppermute(held[-1], 'ctx', ring))  8.47 us
    unnamed x63, local copies, waits for them, and re-layouts  7.29 us
    ppermute x4, waiting for transfers between devices, body(): landed.append(lax.ppermute(results[k], ('pipe', 'ctx'), pairs))  7.09 us
    ppermute x6, starting transfers between devices, ringed(): held.append(lax.ppermute(held[-1], 'ctx', ring))  6.81 us
  transfers between devices with their start and end apart: 26, of which 14 were waited for; matrix products, arithmetic and copies ran while one was open for 4% of the time, Pallas kernels for 14%

profile of v1, /device:TPU:17, one launch (start us, length us, event | category | flops | bytes accessed | tf_op | source)
XLA Modules:
  0.0 113.1 jit_solution(12245071739688218741)
XLA Ops:
  0.0 1.2 %copy.23 = bf16[1,128,1536]{1,2,0:T(8,128)(2,1)S(1)} copy(bf16[1,128,1536]{2,1,0:T(8,128)(2,1)} %param.15) | data formatting | bytes 786432 | tf_op args[2]
  1.6 0.1 copy.24
  1.9 0.7 dynamic-slice_bitcast_fusion
  2.6 1.2 %collective-permute-start.4 = (bf16[128,384]{1,0:T(8,128)(2,1)S(1)}, bf16[128,384]{1,0:T(8,128)(2,1)S(1)}, u32[]{:S(2)}, u32[]{:S(2)}) collective-permute-start(bf16[128,384]{1,0:T(8,128)(2,1)S(1)} %get-tuple-element.73), channel_id=1, source_target_pairs={{0,1},{1,0},{2,3},{3,2},{4,5},{5,4},{6,7},{7,6},{8,9},{9,8},{10,11... | collective-permute-start | bytes 294920 | tf_op jit(solution)/shard_map/ppermute | solution.py:234
  3.8 1.2 %collective-permute-start.5 = (bf16[128,384]{1,0:T(8,128)(2,1)S(1)}, bf16[128,384]{1,0:T(8,128)(2,1)S(1)}, u32[]{:S(2)}, u32[]{:S(2)}) collective-permute-start(bf16[128,384]{1,0:T(8,128)(2,1)S(1)} %get-tuple-element.72), channel_id=1, source_target_pairs={{0,2},{1,3},{2,0},{3,1},{4,6},{5,7},{6,4},{7,5},{8,10},{9,11},{10,... | collective-permute-start | bytes 294920 | tf_op jit(solution)/shard_map/ppermute | solution.py:234
  5.0 0.2 collective-permute-start.6
  5.4 0.6 collective-permute-done.4.b1
  6.1 1.4 %collective-permute-done.5.b2 = bf16[128,384]{1,0:T(8,128)(2,1)S(1)} collective-permute-done((bf16[128,384]{1,0:T(8,128)(2,1)S(1)}, bf16[128,384]{1,0:T(8,128)(2,1)S(1)}, u32[]{:S(2)}, u32[]{:S(2)}) %collective-permute-start.5) | collective-permute-done | bytes 98336 | tf_op jit(solution)/shard_map/ppermute | solution.py:234
  7.5 2.0 %collective-permute-done.6.b3 = bf16[128,384]{1,0:T(8,128)(2,1)S(1)} collective-permute-done((bf16[128,384]{1,0:T(8,128)(2,1)S(1)}, bf16[128,384]{1,0:T(8,128)(2,1)S(1)}, u32[]{:S(2)}, u32[]{:S(2)}) %collective-permute-start.6) | collective-permute-done | bytes 98336 | tf_op jit(solution)/shard_map/ppermute | solution.py:234
  9.5 0.6 copy-done.21
  10.1 1.8 %shard_map.56.refs_0_ = bf16[512,384]{1,0:T(8,128)(2,1)} custom-call(s32[64]{0:T(128)} %copy-done.25, bf16[128,384]{1,0:T(8,128)(2,1)} %get-tuple-element.74.b0, bf16[128,384]{1,0:T(8,128)(2,1)} %copy-done.19, bf16[128,384]{1,0:T(8,128)(2,1)} %copy-done.20, bf16[128,384]{1,0:T(8,128)(2,1)} %copy-done.21), custom_call_target="tpu_custom_call" | custom-call | bytes 786432 | tf_op jit(solution)/shard_map/pallas_call | solution.py:26
  12.0 1.3 %collective-permute-start.7 = (bf16[512,384]{1,0:T(8,128)(2,1)}, bf16[512,384]{1,0:T(8,128)(2,1)S(1)}, u32[]{:S(2)}, u32[]{:S(2)}) collective-permute-start(bf16[512,384]{1,0:T(8,128)(2,1)} %shard_map.56.refs_0_), channel_id=1, source_target_pairs={{0,8},{1,9},{2,10},{3,11},{8,12},{9,13},{10,14},{11,15},{12,4},{13... | collective-permute-start | bytes 1179656 | tf_op jit(solution)/shard_map/ppermute | solution.py:249
  13.3 1.3 %collective-permute-start = (bf16[128,2048]{1,0:T(8,128)(2,1)S(1)}, bf16[128,2048]{1,0:T(8,128)(2,1)S(1)}, u32[]{:S(2)}, u32[]{:S(2)}) collective-permute-start(bf16[128,2048]{1,0:T(8,128)(2,1)S(1)} %bitcast.42), channel_id=1, source_target_pairs={{0,1},{1,0},{2,3},{3,2},{4,5},{5,4},{6,7},{7,6},{8,9},{9,8},{10,11... | collective-permute-start | bytes 1572872 | tf_op jit(solution)/shard_map/ppermute | solution.py:234
  14.6 0.2 collective-permute-start.1
  14.8 0.2 reshape_squeeze.3
  15.0 0.6 constant_dynamic-slice_fusion.3
  15.6 0.2 collective-permute-start.16
  15.8 1.3 %collective-permute-start.17 = (bf16[64,512]{1,0:T(8,128)(2,1)S(1)}, bf16[64,512]{1,0:T(8,128)(2,1)S(1)}, u32[]{:S(2)}, u32[]{:S(2)}) collective-permute-start(bf16[64,512]{1,0:T(8,128)(2,1)S(1)} %bitcast.47), channel_id=1, source_target_pairs={{0,2},{1,3},{2,0},{3,1},{4,6},{5,7},{6,4},{7,5},{8,10},{9,11},{10,... | collective-permute-start | bytes 196616 | tf_op jit(solution)/shard_map/ppermute | solution.py:234
  17.1 4.3 %collective-permute-done.7.refs_1_ = bf16[512,384]{1,0:T(8,128)(2,1)S(1)} collective-permute-done((bf16[512,384]{1,0:T(8,128)(2,1)}, bf16[512,384]{1,0:T(8,128)(2,1)S(1)}, u32[]{:S(2)}, u32[]{:S(2)}) %collective-permute-start.7) | collective-permute-done | bytes 393248 | tf_op jit(solution)/shard_map/ppermute | solution.py:249
  21.5 0.4 collective-permute-start.8
  21.9 0.2 reduce-window.8
  22.2 3.5 %collective-permute-done.16.b1 = bf16[64,512]{1,0:T(8,128)(2,1)S(1)} collective-permute-done((bf16[64,512]{1,0:T(8,128)(2,1)S(1)}, bf16[64,512]{1,0:T(8,128)(2,1)S(1)}, u32[]{:S(2)}, u32[]{:S(2)}) %collective-permute-start.16) | collective-permute-done | bytes 65568 | tf_op jit(solution)/shard_map/ppermute | solution.py:234
  25.6 1.6 %collective-permute-start.18 = (bf16[64,512]{1,0:T(8,128)(2,1)S(1)}, bf16[64,512]{1,0:T(8,128)(2,1)S(1)}, u32[]{:S(2)}, u32[]{:S(2)}) collective-permute-start(bf16[64,512]{1,0:T(8,128)(2,1)S(1)} %bitcast.49), channel_id=1, source_target_pairs={{0,3},{1,2},{2,1},{3,0},{4,7},{5,6},{6,5},{7,4},{8,11},{9,10},{10,... | collective-permute-start | bytes 196616 | tf_op jit(solution)/shard_map/ppermute | solution.py:234
  27.3 2.6 %collective-permute-done.8.refs_2_ = bf16[512,384]{1,0:T(8,128)(2,1)S(1)} collective-permute-done((bf16[512,384]{1,0:T(8,128)(2,1)S(1)}, bf16[512,384]{1,0:T(8,128)(2,1)S(1)}, u32[]{:S(2)}, u32[]{:S(2)}) %collective-permute-start.8) | collective-permute-done | bytes 393248 | tf_op jit(solution)/shard_map/ppermute | solution.py:249
  29.9 0.7 copy.44
  30.6 0.6 copy-done.23
  31.3 1.7 %shard_map.59.refs_0_ = bf16[256,512]{1,0:T(8,128)(2,1)} custom-call(s32[64]{0:T(128)} %copy-done.25, bf16[64,512]{1,0:T(8,128)(2,1)} %bitcast.44, bf16[64,512]{1,0:T(8,128)(2,1)} %copy-done.22, bf16[64,512]{1,0:T(8,128)(2,1)} %copy-done.23, bf16[64,512]{1,0:T(8,128)(2,1)} %copy-done.24), custom_call_target="tpu_custom_call" | custom-call | bytes 524288 | tf_op jit(solution)/shard_map/pallas_call | solution.py:26
  33.0 1.3 %collective-permute-start.19 = (bf16[256,512]{1,0:T(8,128)(2,1)}, bf16[256,512]{1,0:T(8,128)(2,1)}, u32[]{:S(2)}, u32[]{:S(2)}) collective-permute-start(bf16[256,512]{1,0:T(8,128)(2,1)} %shard_map.59.refs_0_), channel_id=1, source_target_pairs={{0,8},{1,9},{2,10},{3,11},{8,12},{9,13},{10,14},{11,15},{12,4},{13... | collective-permute-start | bytes 786440 | tf_op jit(solution)/shard_map/ppermute | solution.py:249
  34.4 0.9 slice.72
  35.2 3.2 %collective-permute-start.3 = (bf16[64,2048]{1,0:T(8,128)(2,1)}, bf16[64,2048]{1,0:T(8,128)(2,1)S(1)}, u32[]{:S(2)}, u32[]{:S(2)}) collective-permute-start(bf16[64,2048]{1,0:T(8,128)(2,1)} %slice.72), channel_id=1, source_target_pairs={{0,1},{1,0},{2,3},{3,2},{4,5},{5,4},{6,7},{7,6},{8,9},{9,8},{10,11... | collective-permute-start | bytes 786440 | tf_op jit(solution)/shard_map/ppermute | solution.py:234
  38.4 0.3 fusion
  38.8 0.8 copy.27.cos_ref
  39.6 0.9 copy.28.sin_ref
  40.5 2.2 %collective-permute-done.3.x3b = bf16[64,2048]{1,0:T(8,128)(2,1)S(1)} collective-permute-done((bf16[64,2048]{1,0:T(8,128)(2,1)}, bf16[64,2048]{1,0:T(8,128)(2,1)S(1)}, u32[]{:S(2)}, u32[]{:S(2)}) %collective-permute-start.3) | collective-permute-done | bytes 262176 | tf_op jit(solution)/shard_map/ppermute | solution.py:234
  42.7 0.7 copy-done.9
  43.4 3.8 %shard_map.55 = (bf16[512,2048]{1,0:T(8,128)(2,1)}, bf16[512,512]{1,0:T(8,128)(2,1)}) custom-call(s32[64]{0:T(128)} %copy-done.25, bf16[128,2048]{1,0:T(8,128)(2,1)} %bitcast.41, bf16[128,2048]{1,0:T(8,128)(2,1)} %copy-done, bf16[128,2048]{1,0:T(8,128)(2,1)} %copy-done.1, bf16[64,2048]{1,0:T(8,128)(2,1)} %copy-done.8, bf16[64,2048]{1,0:T(8,128)(2,1)} %copy-done.9, ...), custom_call_target="tpu_custom_call" | custom-call | bytes 4194304 | tf_op jit(solution)/shard_map/pallas_call | solution.py:26
  47.2 0.7 copy-done.7
  48.0 4.5 %shard_map.57 = (bf16[512,256]{1,0:T(8,128)(2,1)}, bf16[512,128]{1,0:T(8,128)(2,1)}) custom-call(s32[64]{0:T(128)} %copy-done.25, bf16[512,2048]{1,0:T(8,128)(2,1)} %get-tuple-element.61.normed_ref, f32[512,128]{1,0:T(8,128)} %copy.27.cos_ref, f32[512,128]{1,0:T(8,128)} %copy.28.sin_ref, bf16[512,384]{1,0:T(8,128)(2,1)} %shard_map.56.refs_0_, ...), custom_call_target="tpu_custom_call" | custom-call | flops 805306368 | bytes 3670016 | tf_op jit(solution)/shard_map/pallas_call | solution.py:26
  52.4 1.3 %collective-permute-start.10 = (bf16[512,128]{1,0:T(8,128)(2,1)}, bf16[512,128]{1,0:T(8,128)(2,1)S(1)}, u32[]{:S(2)}, u32[]{:S(2)}) collective-permute-start(bf16[512,128]{1,0:T(8,128)(2,1)} %get-tuple-element.63.refs_2_), channel_id=1, source_target_pairs={{0,8},{1,9},{2,10},{3,11},{4,12},{5,13},{6,14},{7,15},{16,24},{17,... | collective-permute-start | bytes 393224 | tf_op jit(solution)/shard_map/ppermute | solution.py:314
  53.7 2.0 %collective-permute-start.11 = (bf16[512,128]{1,0:T(8,128)(2,1)}, bf16[512,128]{1,0:T(8,128)(2,1)S(1)}, u32[]{:S(2)}, u32[]{:S(2)}) collective-permute-start(bf16[512,128]{1,0:T(8,128)(2,1)} %get-tuple-element.63.refs_2_), channel_id=1, source_target_pairs={{0,4},{1,5},{2,6},{3,7},{4,8},{5,9},{6,10},{7,11},{8,12},{9,13},{1... | collective-permute-start | bytes 393224 | tf_op jit(solution)/shard_map/ppermute | solution.py:314
  55.8 3.6 %collective-permute-done.10.refs_0_ = bf16[512,128]{1,0:T(8,128)(2,1)S(1)} collective-permute-done((bf16[512,128]{1,0:T(8,128)(2,1)}, bf16[512,128]{1,0:T(8,128)(2,1)S(1)}, u32[]{:S(2)}, u32[]{:S(2)}) %collective-permute-start.10) | collective-permute-done | bytes 131104 | tf_op jit(solution)/shard_map/ppermute | solution.py:314
  59.3 1.6 %collective-permute-done.11.refs_1_ = bf16[512,128]{1,0:T(8,128)(2,1)S(1)} collective-permute-done((bf16[512,128]{1,0:T(8,128)(2,1)}, bf16[512,128]{1,0:T(8,128)(2,1)S(1)}, u32[]{:S(2)}, u32[]{:S(2)}) %collective-permute-start.11) | collective-permute-done | bytes 131104 | tf_op jit(solution)/shard_map/ppermute | solution.py:314
  60.9 0.6 copy-done.28
  61.6 6.4 %shard_map.58.a0 = bf16[512,256]{1,0:T(8,128)(2,1)} custom-call(s32[64]{0:T(128)} %copy-done.25, bf16[512,256]{1,0:T(8,128)(2,1)} %get-tuple-element.62.q_ref, bf16[512,128]{1,0:T(8,128)(2,1)} %copy-done.27, bf16[512,128]{1,0:T(8,128)(2,1)} %copy-done.28, bf16[512,128]{1,0:T(8,128)(2,1)} %get-tuple-element.63.refs_2_), custom_call_target="tpu_custom_call" | custom-call | flops 536870912 | bytes 524288 | tf_op jit(solution)/shard_map/pallas_call | solution.py:26
  68.0 1.4 %collective-permute-start.12 = (bf16[512,256]{1,0:T(8,128)(2,1)}, bf16[512,256]{1,0:T(8,128)(2,1)S(1)}, u32[]{:S(2)}, u32[]{:S(2)}) collective-permute-start(bf16[512,256]{1,0:T(8,128)(2,1)} %shard_map.58.a0), channel_id=1, source_target_pairs={{0,1},{1,0},{2,3},{3,2},{4,5},{5,4},{6,7},{7,6},{8,9},{9,8},{10,11... | collective-permute-start | bytes 786440 | tf_op jit(solution)/shard_map/ppermute | solution.py:234
  69.5 1.4 %collective-permute-start.13 = (bf16[512,256]{1,0:T(8,128)(2,1)}, bf16[512,256]{1,0:T(8,128)(2,1)S(1)}, u32[]{:S(2)}, u32[]{:S(2)}) collective-permute-start(bf16[512,256]{1,0:T(8,128)(2,1)} %shard_map.58.a0), channel_id=1, source_target_pairs={{0,2},{1,3},{2,0},{3,1},{4,6},{5,7},{6,4},{7,5},{8,10},{9,11},{10,... | collective-permute-start | bytes 786440 | tf_op jit(solution)/shard_map/ppermute | solution.py:234
  70.8 3.8 %collective-permute-start.21 = (bf16[256,512]{1,0:T(8,128)(2,1)S(1)}, bf16[256,512]{1,0:T(8,128)(2,1)S(1)}, u32[]{:S(2)}, u32[]{:S(2)}) collective-permute-start(bf16[256,512]{1,0:T(8,128)(2,1)S(1)} %collective-permute-done.20.refs_2_), channel_id=1, source_target_pairs={{0,8},{1,9},{2,10},{3,11},{8,12},{9,13},{10,14},{11,15},{12,4},{13... | collective-permute-start | bytes 786440 | tf_op jit(solution)/shard_map/ppermute | solution.py:249
  74.6 0.3 collective-permute-start.14
  74.9 1.5 %collective-permute-start.15 = (bf16[256,256]{1,0:T(8,128)(2,1)S(1)}, bf16[256,256]{1,0:T(8,128)(2,1)S(1)}, u32[]{:S(2)}, u32[]{:S(2)}) collective-permute-start(bf16[256,256]{1,0:T(8,128)(2,1)S(1)} %slice.77), channel_id=1, source_target_pairs={{0,1},{1,0},{2,3},{3,2},{4,5},{5,4},{6,7},{7,6},{8,9},{9,8},{10,11... | collective-permute-start | bytes 393224 | tf_op jit(solution)/shard_map/ppermute | solution.py:234
  76.4 1.5 %collective-permute-done.21.refs_3_ = bf16[256,512]{1,0:T(8,128)(2,1)S(1)} collective-permute-done((bf16[256,512]{1,0:T(8,128)(2,1)S(1)}, bf16[256,512]{1,0:T(8,128)(2,1)S(1)}, u32[]{:S(2)}, u32[]{:S(2)}) %collective-permute-start.21) | collective-permute-done | bytes 262176 | tf_op jit(solution)/shard_map/ppermute | solution.py:249
  77.9 0.6 collective-permute-done.14.a3a
  78.5 0.3 collective-permute-done.15.a3b
  78.8 0.3 copy-done.13
  79.2 0.3 copy-done.14
  79.4 3.1 %shard_map.60 = (bf16[128,512]{1,0:T(8,128)(2,1)}, bf16[128,512]{1,0:T(8,128)(2,1)}, bf16[128,512]{1,0:T(8,128)(2,1)}, bf16[128,512]{1,0:T(8,128)(2,1)}) custom-call(s32[64]{0:T(128)} %copy-done.25, bf16[512,256]{1,0:T(8,128)(2,1)} %shard_map.58.a0, bf16[512,256]{1,0:T(8,128)(2,1)} %copy-done.2, bf16[512,256]{1,0:T(8,128)(2,1)} %copy-done.3, ...), custom_call_target="tpu_custom_call" | custom-call | flops 536870912 | bytes 2097152 | tf_op jit(solution)/shard_map/pallas_call | solution.py:26
  82.6 17.3 %collective-permute-start.22 = (bf16[128,512]{1,0:T(8,128)(2,1)}, bf16[128,512]{1,0:T(8,128)(2,1)S(1)}, u32[]{:S(2)}, u32[]{:S(2)}) collective-permute-start(bf16[128,512]{1,0:T(8,128)(2,1)} %get-tuple-element.65), channel_id=1, source_target_pairs={{0,16},{1,17},{2,18},{3,19},{4,20},{5,21},{6,22},{7,23},{8,24},{9,... | collective-permute-start | bytes 393224 | tf_op jit(solution)/shard_map/ppermute | solution.py:348
  99.9 1.3 %collective-permute-start.23 = (bf16[128,512]{1,0:T(8,128)(2,1)}, bf16[128,512]{1,0:T(8,128)(2,1)S(1)}, u32[]{:S(2)}, u32[]{:S(2)}) collective-permute-start(bf16[128,512]{1,0:T(8,128)(2,1)} %get-tuple-element.66), channel_id=1, source_target_pairs={{0,17},{1,16},{2,19},{3,18},{4,21},{5,20},{6,23},{7,22},{8,25},{9,... | collective-permute-start | bytes 393224 | tf_op jit(solution)/shard_map/ppermute | solution.py:348
  101.2 0.5 collective-permute-start.24
  101.7 1.0 collective-permute-start.25
  102.8 2.8 %collective-permute-done.23.r1 = bf16[128,512]{1,0:T(8,128)(2,1)S(1)} collective-permute-done((bf16[128,512]{1,0:T(8,128)(2,1)}, bf16[128,512]{1,0:T(8,128)(2,1)S(1)}, u32[]{:S(2)}, u32[]{:S(2)}) %collective-permute-start.23) | collective-permute-done | bytes 131104 | tf_op jit(solution)/shard_map/ppermute | solution.py:348
  105.6 4.3 %collective-permute-done.24.r2 = bf16[128,512]{1,0:T(8,128)(2,1)S(1)} collective-permute-done((bf16[128,512]{1,0:T(8,128)(2,1)}, bf16[128,512]{1,0:T(8,128)(2,1)S(1)}, u32[]{:S(2)}, u32[]{:S(2)}) %collective-permute-start.24) | collective-permute-done | bytes 131104 | tf_op jit(solution)/shard_map/ppermute | solution.py:348
  109.9 0.6 copy-done.17
  110.5 0.6 copy-done.18
  111.2 1.9 %shard_map.61 = bf16[128,2048]{1,0:T(8,128)(2,1)} custom-call(s32[64]{0:T(128)} %copy-done.25, bf16[128,512]{1,0:T(8,128)(2,1)} %copy-done.15, bf16[128,512]{1,0:T(8,128)(2,1)} %copy-done.16, bf16[128,512]{1,0:T(8,128)(2,1)} %copy-done.17, bf16[128,512]{1,0:T(8,128)(2,1)} %copy-done.18), custom_call_target="tpu_custom_call" | custom-call | bytes 1048576 | tf_op jit(solution)/shard_map/pallas_call | solution.py:26
  (87 shorter events, 1.1 us)
Async XLA Ops:
  0.0 5.4 %copy-start.26 = (s32[2,4]{1,0:T(2,128)S(1)}, s32[2,4]{1,0:T(2,128)}, u32[]{:S(2)}) copy-start(s32[2,4]{1,0:T(2,128)} %param.17) | copy-start | bytes 100
  1.2 12.0 %copy-start.4 = (bf16[1,128,2048]{2,1,0:T(8,128)(2,1)S(1)}, bf16[1,128,2048]{2,1,0:T(8,128)(2,1)}, u32[]{:S(2)}) copy-start(bf16[1,128,2048]{2,1,0:T(8,128)(2,1)} %param.13) | copy-start | bytes 1572868
  1.2 13.5 %copy-start.10 = (bf16[1,64,2048]{2,1,0:T(8,128)(2,1)S(1)}, bf16[1,64,2048]{2,1,0:T(8,128)(2,1)}, u32[]{:S(2)}) copy-start(bf16[1,64,2048]{2,1,0:T(8,128)(2,1)} %param.16) | copy-start | bytes 786436
  2.6 3.5 %collective-permute-start.4 = (bf16[128,384]{1,0:T(8,128)(2,1)S(1)}, bf16[128,384]{1,0:T(8,128)(2,1)S(1)}, u32[]{:S(2)}, u32[]{:S(2)}) collective-permute-start(bf16[128,384]{1,0:T(8,128)(2,1)S(1)} %get-tuple-element.73), channel_id=1, source_target_pairs={{0,1},{1,0},{2,3},{3,2},{4,5},{5,4},{6,7},{7,6},{8,9},{9,8},{10,11... | collective-permute-start | bytes 294920 | tf_op jit(solution)/shard_map/ppermute | solution.py:234
  3.8 3.7 %collective-permute-start.5 = (bf16[128,384]{1,0:T(8,128)(2,1)S(1)}, bf16[128,384]{1,0:T(8,128)(2,1)S(1)}, u32[]{:S(2)}, u32[]{:S(2)}) collective-permute-start(bf16[128,384]{1,0:T(8,128)(2,1)S(1)} %get-tuple-element.72), channel_id=1, source_target_pairs={{0,2},{1,3},{2,0},{3,1},{4,6},{5,7},{6,4},{7,5},{8,10},{9,11},{10,... | collective-permute-start | bytes 294920 | tf_op jit(solution)/shard_map/ppermute | solution.py:234
  5.0 4.5 %collective-permute-start.6 = (bf16[128,384]{1,0:T(8,128)(2,1)S(1)}, bf16[128,384]{1,0:T(8,128)(2,1)S(1)}, u32[]{:S(2)}, u32[]{:S(2)}) collective-permute-start(bf16[128,384]{1,0:T(8,128)(2,1)S(1)} %get-tuple-element.71), channel_id=1, source_target_pairs={{0,3},{1,2},{2,1},{3,0},{4,7},{5,6},{6,5},{7,4},{8,11},{9,10},{10,... | collective-permute-start | bytes 294920 | tf_op jit(solution)/shard_map/ppermute | solution.py:234
  5.4 4.1 %copy-start.25 = (s32[64]{0:T(128)}, s32[64]{0:T(128)S(1)}, u32[]{:S(2)}) copy-start(s32[64]{0:T(128)S(1)} %get-tuple-element.69.s_ref) | copy-start | bytes 772
  6.1 3.5 %copy-start.19 = (bf16[128,384]{1,0:T(8,128)(2,1)}, bf16[128,384]{1,0:T(8,128)(2,1)S(1)}, u32[]{:S(2)}) copy-start(bf16[128,384]{1,0:T(8,128)(2,1)S(1)} %collective-permute-done.4.b1) | copy-start | bytes 294916
  7.5 2.0 %copy-start.20 = (bf16[128,384]{1,0:T(8,128)(2,1)}, bf16[128,384]{1,0:T(8,128)(2,1)S(1)}, u32[]{:S(2)}) copy-start(bf16[128,384]{1,0:T(8,128)(2,1)S(1)} %collective-permute-done.5.b2) | copy-start | bytes 294916
  9.5 0.6 copy-start.21
  12.0 9.5 %collective-permute-start.7 = (bf16[512,384]{1,0:T(8,128)(2,1)}, bf16[512,384]{1,0:T(8,128)(2,1)S(1)}, u32[]{:S(2)}, u32[]{:S(2)}) collective-permute-start(bf16[512,384]{1,0:T(8,128)(2,1)} %shard_map.56.refs_0_), channel_id=1, source_target_pairs={{0,8},{1,9},{2,10},{3,11},{8,12},{9,13},{10,14},{11,15},{12,4},{13... | collective-permute-start | bytes 1179656 | tf_op jit(solution)/shard_map/ppermute | solution.py:249
  13.3 21.0 %collective-permute-start = (bf16[128,2048]{1,0:T(8,128)(2,1)S(1)}, bf16[128,2048]{1,0:T(8,128)(2,1)S(1)}, u32[]{:S(2)}, u32[]{:S(2)}) collective-permute-start(bf16[128,2048]{1,0:T(8,128)(2,1)S(1)} %bitcast.42), channel_id=1, source_target_pairs={{0,1},{1,0},{2,3},{3,2},{4,5},{5,4},{6,7},{7,6},{8,9},{9,8},{10,11... | collective-permute-start | bytes 1572872 | tf_op jit(solution)/shard_map/ppermute | solution.py:234
  14.6 19.8 %collective-permute-start.1 = (bf16[128,2048]{1,0:T(8,128)(2,1)S(1)}, bf16[128,2048]{1,0:T(8,128)(2,1)S(1)}, u32[]{:S(2)}, u32[]{:S(2)}) collective-permute-start(bf16[128,2048]{1,0:T(8,128)(2,1)S(1)} %bitcast.43), channel_id=1, source_target_pairs={{0,2},{1,3},{2,0},{3,1},{4,6},{5,7},{6,4},{7,5},{8,10},{9,11},{10,... | collective-permute-start | bytes 1572872 | tf_op jit(solution)/shard_map/ppermute | solution.py:234
  15.6 10.1 %collective-permute-start.16 = (bf16[64,512]{1,0:T(8,128)(2,1)S(1)}, bf16[64,512]{1,0:T(8,128)(2,1)S(1)}, u32[]{:S(2)}, u32[]{:S(2)}) collective-permute-start(bf16[64,512]{1,0:T(8,128)(2,1)S(1)} %bitcast.48), channel_id=1, source_target_pairs={{0,1},{1,0},{2,3},{3,2},{4,5},{5,4},{6,7},{7,6},{8,9},{9,8},{10,11... | collective-permute-start | bytes 196616 | tf_op jit(solution)/shard_map/ppermute | solution.py:234
  15.8 14.8 %collective-permute-start.17 = (bf16[64,512]{1,0:T(8,128)(2,1)S(1)}, bf16[64,512]{1,0:T(8,128)(2,1)S(1)}, u32[]{:S(2)}, u32[]{:S(2)}) collective-permute-start(bf16[64,512]{1,0:T(8,128)(2,1)S(1)} %bitcast.47), channel_id=1, source_target_pairs={{0,2},{1,3},{2,0},{3,1},{4,6},{5,7},{6,4},{7,5},{8,10},{9,11},{10,... | collective-permute-start | bytes 196616 | tf_op jit(solution)/shard_map/ppermute | solution.py:234
  21.5 19.0 %copy-start.5 = (bf16[512,384]{1,0:T(8,128)(2,1)}, bf16[512,384]{1,0:T(8,128)(2,1)S(1)}, u32[]{:S(2)}) copy-start(bf16[512,384]{1,0:T(8,128)(2,1)S(1)} %collective-permute-done.7.refs_1_) | copy-start | bytes 1179652
  21.5 8.4 %collective-permute-start.8 = (bf16[512,384]{1,0:T(8,128)(2,1)S(1)}, bf16[512,384]{1,0:T(8,128)(2,1)S(1)}, u32[]{:S(2)}, u32[]{:S(2)}) collective-permute-start(bf16[512,384]{1,0:T(8,128)(2,1)S(1)} %collective-permute-done.7.refs_1_), channel_id=1, source_target_pairs={{0,8},{1,9},{2,10},{3,11},{8,12},{9,13},{10,14},{11,15},{12,4},{13... | collective-permute-start | bytes 1179656 | tf_op jit(solution)/shard_map/ppermute | solution.py:249
  25.6 5.0 %copy-start.22 = (bf16[64,512]{1,0:T(8,128)(2,1)}, bf16[64,512]{1,0:T(8,128)(2,1)S(1)}, u32[]{:S(2)}) copy-start(bf16[64,512]{1,0:T(8,128)(2,1)S(1)} %collective-permute-done.16.b1) | copy-start | bytes 196612
  25.6 5.0 %collective-permute-start.18 = (bf16[64,512]{1,0:T(8,128)(2,1)S(1)}, bf16[64,512]{1,0:T(8,128)(2,1)S(1)}, u32[]{:S(2)}, u32[]{:S(2)}) collective-permute-start(bf16[64,512]{1,0:T(8,128)(2,1)S(1)} %bitcast.49), channel_id=1, source_target_pairs={{0,3},{1,2},{2,1},{3,0},{4,7},{5,6},{6,5},{7,4},{8,11},{9,10},{10,... | collective-permute-start | bytes 196616 | tf_op jit(solution)/shard_map/ppermute | solution.py:234
  29.9 17.3 %copy-start.6 = (bf16[512,384]{1,0:T(8,128)(2,1)}, bf16[512,384]{1,0:T(8,128)(2,1)S(1)}, u32[]{:S(2)}) copy-start(bf16[512,384]{1,0:T(8,128)(2,1)S(1)} %collective-permute-done.8.refs_2_) | copy-start | bytes 1179652
  29.9 17.3 %collective-permute-start.9 = (bf16[512,384]{1,0:T(8,128)(2,1)S(1)}, bf16[512,384]{1,0:T(8,128)(2,1)S(1)}, u32[]{:S(2)}, u32[]{:S(2)}) collective-permute-start(bf16[512,384]{1,0:T(8,128)(2,1)S(1)} %collective-permute-done.8.refs_2_), channel_id=1, source_target_pairs={{0,8},{1,9},{2,10},{3,11},{8,12},{9,13},{10,14},{11,15},{12,4},{13... | collective-permute-start | bytes 1179656 | tf_op jit(solution)/shard_map/ppermute | solution.py:249
  30.6 0.6 copy-start.23
  30.6 0.7 copy-start.24
  33.0 22.7 %collective-permute-start.19 = (bf16[256,512]{1,0:T(8,128)(2,1)}, bf16[256,512]{1,0:T(8,128)(2,1)}, u32[]{:S(2)}, u32[]{:S(2)}) collective-permute-start(bf16[256,512]{1,0:T(8,128)(2,1)} %shard_map.59.refs_0_), channel_id=1, source_target_pairs={{0,8},{1,9},{2,10},{3,11},{8,12},{9,13},{10,14},{11,15},{12,4},{13... | collective-permute-start | bytes 786440 | tf_op jit(solution)/shard_map/ppermute | solution.py:249
  34.2 8.4 %copy-start = (bf16[128,2048]{1,0:T(8,128)(2,1)}, bf16[128,2048]{1,0:T(8,128)(2,1)S(1)}, u32[]{:S(2)}) copy-start(bf16[128,2048]{1,0:T(8,128)(2,1)S(1)} %collective-permute-done.x1) | copy-start | bytes 1572868
  34.3 6.2 %collective-permute-start.2 = (bf16[64,2048]{1,0:T(8,128)(2,1)S(1)}, bf16[64,2048]{1,0:T(8,128)(2,1)S(1)}, u32[]{:S(2)}, u32[]{:S(2)}) collective-permute-start(bf16[64,2048]{1,0:T(8,128)(2,1)S(1)} %slice.71), channel_id=1, source_target_pairs={{0,2},{1,3},{2,0},{3,1},{4,6},{5,7},{6,4},{7,5},{8,10},{9,11},{10,... | collective-permute-start | bytes 786440 | tf_op jit(solution)/shard_map/ppermute | solution.py:234
  34.4 8.3 %copy-start.1 = (bf16[128,2048]{1,0:T(8,128)(2,1)}, bf16[128,2048]{1,0:T(8,128)(2,1)S(1)}, u32[]{:S(2)}) copy-start(bf16[128,2048]{1,0:T(8,128)(2,1)S(1)} %collective-permute-done.1.x2) | copy-start | bytes 1572868
  35.2 7.5 %collective-permute-start.3 = (bf16[64,2048]{1,0:T(8,128)(2,1)}, bf16[64,2048]{1,0:T(8,128)(2,1)S(1)}, u32[]{:S(2)}, u32[]{:S(2)}) collective-permute-start(bf16[64,2048]{1,0:T(8,128)(2,1)} %slice.72), channel_id=1, source_target_pairs={{0,1},{1,0},{2,3},{3,2},{4,5},{5,4},{6,7},{7,6},{8,9},{9,8},{10,11... | collective-permute-start | bytes 786440 | tf_op jit(solution)/shard_map/ppermute | solution.py:234
  40.5 2.2 %copy-start.8 = (bf16[64,2048]{1,0:T(8,128)(2,1)}, bf16[64,2048]{1,0:T(8,128)(2,1)S(1)}, u32[]{:S(2)}) copy-start(bf16[64,2048]{1,0:T(8,128)(2,1)S(1)} %collective-permute-done.2.x3a) | copy-start | bytes 786436
  42.7 0.7 copy-start.9
  47.2 0.7 copy-start.7
  52.4 6.9 %collective-permute-start.10 = (bf16[512,128]{1,0:T(8,128)(2,1)}, bf16[512,128]{1,0:T(8,128)(2,1)S(1)}, u32[]{:S(2)}, u32[]{:S(2)}) collective-permute-start(bf16[512,128]{1,0:T(8,128)(2,1)} %get-tuple-element.63.refs_2_), channel_id=1, source_target_pairs={{0,8},{1,9},{2,10},{3,11},{4,12},{5,13},{6,14},{7,15},{16,24},{17,... | collective-permute-start | bytes 393224 | tf_op jit(solution)/shard_map/ppermute | solution.py:314
  53.7 7.2 %collective-permute-start.11 = (bf16[512,128]{1,0:T(8,128)(2,1)}, bf16[512,128]{1,0:T(8,128)(2,1)S(1)}, u32[]{:S(2)}, u32[]{:S(2)}) collective-permute-start(bf16[512,128]{1,0:T(8,128)(2,1)} %get-tuple-element.63.refs_2_), channel_id=1, source_target_pairs={{0,4},{1,5},{2,6},{3,7},{4,8},{5,9},{6,10},{7,11},{8,12},{9,13},{1... | collective-permute-start | bytes 393224 | tf_op jit(solution)/shard_map/ppermute | solution.py:314
  55.7 15.1 %collective-permute-start.20 = (bf16[256,512]{1,0:T(8,128)(2,1)}, bf16[256,512]{1,0:T(8,128)(2,1)S(1)}, u32[]{:S(2)}, u32[]{:S(2)}) collective-permute-start(bf16[256,512]{1,0:T(8,128)(2,1)} %collective-permute-done.19.refs_1_), channel_id=1, source_target_pairs={{0,8},{1,9},{2,10},{3,11},{8,12},{9,13},{10,14},{11,15},{12,4},{13... | collective-permute-start | bytes 786440 | tf_op jit(solution)/shard_map/ppermute | solution.py:249
  59.3 1.6 %copy-start.27 = (bf16[512,128]{1,0:T(8,128)(2,1)}, bf16[512,128]{1,0:T(8,128)(2,1)S(1)}, u32[]{:S(2)}) copy-start(bf16[512,128]{1,0:T(8,128)(2,1)S(1)} %collective-permute-done.10.refs_0_) | copy-start | bytes 393220
  60.9 0.6 copy-start.28
  68.0 6.6 %collective-permute-start.12 = (bf16[512,256]{1,0:T(8,128)(2,1)}, bf16[512,256]{1,0:T(8,128)(2,1)S(1)}, u32[]{:S(2)}, u32[]{:S(2)}) collective-permute-start(bf16[512,256]{1,0:T(8,128)(2,1)} %shard_map.58.a0), channel_id=1, source_target_pairs={{0,1},{1,0},{2,3},{3,2},{4,5},{5,4},{6,7},{7,6},{8,9},{9,8},{10,11... | collective-permute-start | bytes 786440 | tf_op jit(solution)/shard_map/ppermute | solution.py:234
  69.5 5.4 %collective-permute-start.13 = (bf16[512,256]{1,0:T(8,128)(2,1)}, bf16[512,256]{1,0:T(8,128)(2,1)S(1)}, u32[]{:S(2)}, u32[]{:S(2)}) collective-permute-start(bf16[512,256]{1,0:T(8,128)(2,1)} %shard_map.58.a0), channel_id=1, source_target_pairs={{0,2},{1,3},{2,0},{3,1},{4,6},{5,7},{6,4},{7,5},{8,10},{9,11},{10,... | collective-permute-start | bytes 786440 | tf_op jit(solution)/shard_map/ppermute | solution.py:234
  70.8 8.0 %copy-start.11 = (bf16[256,512]{1,0:T(8,128)(2,1)}, bf16[256,512]{1,0:T(8,128)(2,1)S(1)}, u32[]{:S(2)}) copy-start(bf16[256,512]{1,0:T(8,128)(2,1)S(1)} %collective-permute-done.20.refs_2_) | copy-start | bytes 786436
  70.8 7.1 %collective-permute-start.21 = (bf16[256,512]{1,0:T(8,128)(2,1)S(1)}, bf16[256,512]{1,0:T(8,128)(2,1)S(1)}, u32[]{:S(2)}, u32[]{:S(2)}) collective-permute-start(bf16[256,512]{1,0:T(8,128)(2,1)S(1)} %collective-permute-done.20.refs_2_), channel_id=1, source_target_pairs={{0,8},{1,9},{2,10},{3,11},{8,12},{9,13},{10,14},{11,15},{12,4},{13... | collective-permute-start | bytes 786440 | tf_op jit(solution)/shard_map/ppermute | solution.py:249
  74.6 4.2 %copy-start.2 = (bf16[512,256]{1,0:T(8,128)(2,1)}, bf16[512,256]{1,0:T(8,128)(2,1)S(1)}, u32[]{:S(2)}) copy-start(bf16[512,256]{1,0:T(8,128)(2,1)S(1)} %collective-permute-done.12.a1) | copy-start | bytes 786436
  74.6 3.9 %collective-permute-start.14 = (bf16[256,256]{1,0:T(8,128)(2,1)S(1)}, bf16[256,256]{1,0:T(8,128)(2,1)S(1)}, u32[]{:S(2)}, u32[]{:S(2)}) collective-permute-start(bf16[256,256]{1,0:T(8,128)(2,1)S(1)} %slice.76), channel_id=1, source_target_pairs={{0,2},{1,3},{2,0},{3,1},{4,6},{5,7},{6,4},{7,5},{8,10},{9,11},{10,... | collective-permute-start | bytes 393224 | tf_op jit(solution)/shard_map/ppermute | solution.py:234
  74.9 3.9 %copy-start.3 = (bf16[512,256]{1,0:T(8,128)(2,1)}, bf16[512,256]{1,0:T(8,128)(2,1)S(1)}, u32[]{:S(2)}) copy-start(bf16[512,256]{1,0:T(8,128)(2,1)S(1)} %collective-permute-done.13.a2) | copy-start | bytes 786436
  74.9 3.9 %collective-permute-start.15 = (bf16[256,256]{1,0:T(8,128)(2,1)S(1)}, bf16[256,256]{1,0:T(8,128)(2,1)S(1)}, u32[]{:S(2)}, u32[]{:S(2)}) collective-permute-start(bf16[256,256]{1,0:T(8,128)(2,1)S(1)} %slice.77), channel_id=1, source_target_pairs={{0,1},{1,0},{2,3},{3,2},{4,5},{5,4},{6,7},{7,6},{8,9},{9,8},{10,11... | collective-permute-start | bytes 393224 | tf_op jit(solution)/shard_map/ppermute | solution.py:234
  77.9 0.9 copy-start.12
  78.5 0.6 copy-start.13
  78.8 0.6 copy-start.14
  82.6 20.2 %collective-permute-start.22 = (bf16[128,512]{1,0:T(8,128)(2,1)}, bf16[128,512]{1,0:T(8,128)(2,1)S(1)}, u32[]{:S(2)}, u32[]{:S(2)}) collective-permute-start(bf16[128,512]{1,0:T(8,128)(2,1)} %get-tuple-element.65), channel_id=1, source_target_pairs={{0,16},{1,17},{2,18},{3,19},{4,20},{5,21},{6,22},{7,23},{8,24},{9,... | collective-permute-start | bytes 393224 | tf_op jit(solution)/shard_map/ppermute | solution.py:348
  99.9 5.7 %collective-permute-start.23 = (bf16[128,512]{1,0:T(8,128)(2,1)}, bf16[128,512]{1,0:T(8,128)(2,1)S(1)}, u32[]{:S(2)}, u32[]{:S(2)}) collective-permute-start(bf16[128,512]{1,0:T(8,128)(2,1)} %get-tuple-element.66), channel_id=1, source_target_pairs={{0,17},{1,16},{2,19},{3,18},{4,21},{5,20},{6,23},{7,22},{8,25},{9,... | collective-permute-start | bytes 393224 | tf_op jit(solution)/shard_map/ppermute | solution.py:348
  101.2 8.6 %collective-permute-start.24 = (bf16[128,512]{1,0:T(8,128)(2,1)}, bf16[128,512]{1,0:T(8,128)(2,1)S(1)}, u32[]{:S(2)}, u32[]{:S(2)}) collective-permute-start(bf16[128,512]{1,0:T(8,128)(2,1)} %get-tuple-element.67), channel_id=1, source_target_pairs={{0,18},{1,19},{2,16},{3,17},{4,22},{5,23},{6,20},{7,21},{8,26},{9,... | collective-permute-start | bytes 393224 | tf_op jit(solution)/shard_map/ppermute | solution.py:348
  101.7 8.1 %collective-permute-start.25 = (bf16[128,512]{1,0:T(8,128)(2,1)}, bf16[128,512]{1,0:T(8,128)(2,1)S(1)}, u32[]{:S(2)}, u32[]{:S(2)}) collective-permute-start(bf16[128,512]{1,0:T(8,128)(2,1)} %get-tuple-element.68), channel_id=1, source_target_pairs={{0,19},{1,18},{2,17},{3,16},{4,23},{5,22},{6,21},{7,20},{8,27},{9,... | collective-permute-start | bytes 393224 | tf_op jit(solution)/shard_map/ppermute | solution.py:348
  102.8 7.1 %copy-start.15 = (bf16[128,512]{1,0:T(8,128)(2,1)}, bf16[128,512]{1,0:T(8,128)(2,1)S(1)}, u32[]{:S(2)}) copy-start(bf16[128,512]{1,0:T(8,128)(2,1)S(1)} %collective-permute-done.22.r0) | copy-start | bytes 393220
  105.6 4.3 %copy-start.16 = (bf16[128,512]{1,0:T(8,128)(2,1)}, bf16[128,512]{1,0:T(8,128)(2,1)S(1)}, u32[]{:S(2)}) copy-start(bf16[128,512]{1,0:T(8,128)(2,1)S(1)} %collective-permute-done.23.r1) | copy-start | bytes 393220
  109.8 0.7 copy-start.17
  110.5 0.7 copy-start.18

commit v2 on v1

--- a/solution.py
+++ b/solution.py
@@ -25,13 +25,14 @@
     def run(scalars, *arrays):
         return pl.pallas_call(
             kernel,
-            out_shape=out_shape,
+            out_shape=jax.tree.map(lambda o: VMEM(o.shape, o.dtype), out_shape),
             in_specs=[pl.BlockSpec(memory_space=SMEM)]
             + [pl.BlockSpec(memory_space=VMEM)] * len(arrays),
             out_specs=jax.tree.map(lambda _: pl.BlockSpec(memory_space=VMEM), out_shape),
             scratch_shapes=list(scratch),
+            compiler_params=pltpu.CompilerParams(vmem_limit_bytes=16 << 20),
             cost_estimate=pl.CostEstimate(flops=flops, bytes_accessed=moved, transcendentals=0),
-        )(scalars, *arrays)
+        )(scalars, *[pltpu.with_memory_space_constraint(a, VMEM) for a in arrays])
 
     return run
 

time: 113 us -> 99.1 us (0.88)
  Pallas kernels: 23.3 us -> 13.1 us
  local copies, waits for them, and re-layouts: 11.9 us -> 6.83 us
  starting transfers between devices: 45.5 us -> 48.4 us
  waiting for transfers between devices: 31.3 us -> 29.2 us
  other arithmetic: 0.81 us -> 2.35 us
    pallas_call x7, Pallas kernels: 23.3 us -> 13.1 us  [run(): pl.pallas_call(kernel, out_shape=jax.tree.map(lambda o: VMEM(o.shape, o.d...]
    unnamed x63 -> x14, local copies, waits for them, and re-layouts: 7.29 us -> 2.09 us
    ppermute x4, starting transfers between devices: 20.2 us -> 22.8 us  [body(): landed.append(lax.ppermute(results[k], ('pipe', 'ctx'), pairs))]
    ppermute x14, starting transfers between devices: 15.2 us -> 17 us  [across(): return lax.ppermute(value, 'ctx', [(i, i ^ k) for i in range(count)])]
    ppermute x6, waiting for transfers between devices: 8.47 us -> 6.95 us  [ringed(): held.append(lax.ppermute(held[-1], 'ctx', ring))]
    ppermute x6, starting transfers between devices: 6.81 us -> 5.31 us  [ringed(): held.append(lax.ppermute(held[-1], 'ctx', ring))]
  transfers between devices with their start and end apart: 26 -> 26, of which waited for: 14 -> 15; matrix products, arithmetic and copies ran while one was open for 4% -> 7% of each run, Pallas kernels for 14% -> 10%
where the time goes in v2:
time: 99.1 us; the launch traced here: 100 us
  starting transfers between devices  48.4 us (49%)
  waiting for transfers between devices  29.2 us (29%)
  Pallas kernels  13.1 us (13%)
  local copies, waits for them, and re-layouts  6.83 us (7%)
  other arithmetic  2.35 us (2%)
    ppermute x4, starting transfers between devices, body(): landed.append(lax.ppermute(results[k], ('pipe', 'ctx'), pairs))  22.8 us
    ppermute x14, starting transfers between devices, across(): return lax.ppermute(value, 'ctx', [(i, i ^ k) for i in range(count)])  17 us
    pallas_call x7, Pallas kernels, run(): pl.pallas_call(kernel, out_shape=jax.tree.map(lambda o: VMEM(o.shape, o.d...  13.1 us
    ppermute x14, waiting for transfers between devices, across(): return lax.ppermute(value, 'ctx', [(i, i ^ k) for i in range(count)])  10.4 us
    ppermute x6, waiting for transfers between devices, ringed(): held.append(lax.ppermute(held[-1], 'ctx', ring))  6.95 us
    ppermute x4, waiting for transfers between devices, body(): landed.append(lax.ppermute(results[k], ('pipe', 'ctx'), pairs))  6.88 us
    ppermute x6, starting transfers between devices, ringed(): held.append(lax.ppermute(held[-1], 'ctx', ring))  5.31 us
    ppermute x2, waiting for transfers between devices, body(): history.insert(0, lax.ppermute(keys_values, 'ctx', pairs))  4.94 us
  transfers between devices with their start and end apart: 26, of which 15 were waited for; matrix products, arithmetic and copies ran while one was open for 7% of the time, Pallas kernels for 10%

profile of v2, /device:TPU:17, one launch (start us, length us, event | category | flops | bytes accessed | tf_op | source)
XLA Modules:
  0.0 100.2 jit_solution(17739561488359401800)
XLA Ops:
  0.0 1.2 %copy.23 = bf16[1,128,1536]{1,2,0:T(8,128)(2,1)S(1)} copy(bf16[1,128,1536]{2,1,0:T(8,128)(2,1)} %param.15) | data formatting | bytes 786432 | tf_op args[2]
  1.3 0.1 copy.26
  1.5 0.1 copy.25
  1.6 0.2 copy.24
  1.8 0.1 pad_maximum_fusion
  2.0 1.3 %collective-permute-start.4 = (bf16[128,384]{1,0:T(8,128)(2,1)S(1)}, bf16[128,384]{1,0:T(8,128)(2,1)S(1)}, u32[]{:S(2)}, u32[]{:S(2)}) collective-permute-start(bf16[128,384]{1,0:T(8,128)(2,1)S(1)} %get-tuple-element.73), channel_id=1, source_target_pairs={{0,1},{1,0},{2,3},{3,2},{4,5},{5,4},{6,7},{7,6},{8,9},{9,8},{10,11... | collective-permute-start | bytes 294920 | tf_op jit(solution)/shard_map/ppermute | solution.py:235
  3.2 1.2 %collective-permute-start.5 = (bf16[128,384]{1,0:T(8,128)(2,1)S(1)}, bf16[128,384]{1,0:T(8,128)(2,1)S(1)}, u32[]{:S(2)}, u32[]{:S(2)}) collective-permute-start(bf16[128,384]{1,0:T(8,128)(2,1)S(1)} %get-tuple-element.72), channel_id=1, source_target_pairs={{0,2},{1,3},{2,0},{3,1},{4,6},{5,7},{6,4},{7,5},{8,10},{9,11},{10,... | collective-permute-start | bytes 294920 | tf_op jit(solution)/shard_map/ppermute | solution.py:235
  4.5 0.2 collective-permute-start.6
  4.7 0.1 fusion.2
  4.8 0.1 constant_dynamic-update-slice_fusion
  4.9 0.6 collective-permute-done.4.b1
  5.5 1.4 %collective-permute-done.5.b2 = bf16[128,384]{1,0:T(8,128)(2,1)S(1)} collective-permute-done((bf16[128,384]{1,0:T(8,128)(2,1)S(1)}, bf16[128,384]{1,0:T(8,128)(2,1)S(1)}, u32[]{:S(2)}, u32[]{:S(2)}) %collective-permute-start.5) | collective-permute-done | bytes 98336 | tf_op jit(solution)/shard_map/ppermute | solution.py:235
  6.9 2.0 %collective-permute-done.6.b3 = bf16[128,384]{1,0:T(8,128)(2,1)S(1)} collective-permute-done((bf16[128,384]{1,0:T(8,128)(2,1)S(1)}, bf16[128,384]{1,0:T(8,128)(2,1)S(1)}, u32[]{:S(2)}, u32[]{:S(2)}) %collective-permute-start.6) | collective-permute-done | bytes 98336 | tf_op jit(solution)/shard_map/ppermute | solution.py:235
  8.9 0.6 shard_map.56.refs_0_
  9.5 1.3 %collective-permute-start.7 = (bf16[512,384]{1,0:T(8,128)(2,1)S(1)}, bf16[512,384]{1,0:T(8,128)(2,1)S(1)}, u32[]{:S(2)}, u32[]{:S(2)}) collective-permute-start(bf16[512,384]{1,0:T(8,128)(2,1)S(1)} %shard_map.56.refs_0_), channel_id=1, source_target_pairs={{0,8},{1,9},{2,10},{3,11},{8,12},{9,13},{10,14},{11,15},{12,4},{13... | collective-permute-start | bytes 1179656 | tf_op jit(solution)/shard_map/ppermute | solution.py:250
  10.9 1.3 %collective-permute-start = (bf16[128,2048]{1,0:T(8,128)(2,1)S(1)}, bf16[128,2048]{1,0:T(8,128)(2,1)S(1)}, u32[]{:S(2)}, u32[]{:S(2)}) collective-permute-start(bf16[128,2048]{1,0:T(8,128)(2,1)S(1)} %bitcast.37), channel_id=1, source_target_pairs={{0,1},{1,0},{2,3},{3,2},{4,5},{5,4},{6,7},{7,6},{8,9},{9,8},{10,11... | collective-permute-start | bytes 1572872 | tf_op jit(solution)/shard_map/ppermute | solution.py:235
  12.2 0.2 collective-permute-start.1
  12.4 0.2 reshape_squeeze.3
  12.6 0.6 constant_dynamic-slice_fusion.3
  13.2 0.2 collective-permute-start.16
  13.4 1.3 %collective-permute-start.17 = (bf16[64,512]{1,0:T(8,128)(2,1)S(1)}, bf16[64,512]{1,0:T(8,128)(2,1)S(1)}, u32[]{:S(2)}, u32[]{:S(2)}) collective-permute-start(bf16[64,512]{1,0:T(8,128)(2,1)S(1)} %bitcast.48), channel_id=1, source_target_pairs={{0,2},{1,3},{2,0},{3,1},{4,6},{5,7},{6,4},{7,5},{8,10},{9,11},{10,... | collective-permute-start | bytes 196616 | tf_op jit(solution)/shard_map/ppermute | solution.py:235
  14.7 4.1 %collective-permute-done.7.refs_1_ = bf16[512,384]{1,0:T(8,128)(2,1)S(1)} collective-permute-done((bf16[512,384]{1,0:T(8,128)(2,1)S(1)}, bf16[512,384]{1,0:T(8,128)(2,1)S(1)}, u32[]{:S(2)}, u32[]{:S(2)}) %collective-permute-start.7) | collective-permute-done | bytes 393248 | tf_op jit(solution)/shard_map/ppermute | solution.py:250
  18.9 0.4 collective-permute-start.8
  19.3 0.2 reduce-window.8
  19.4 0.1 select_reduce_fusion
  19.6 3.7 %collective-permute-done.16.b1 = bf16[64,512]{1,0:T(8,128)(2,1)S(1)} collective-permute-done((bf16[64,512]{1,0:T(8,128)(2,1)S(1)}, bf16[64,512]{1,0:T(8,128)(2,1)S(1)}, u32[]{:S(2)}, u32[]{:S(2)}) %collective-permute-start.16) | collective-permute-done | bytes 65568 | tf_op jit(solution)/shard_map/ppermute | solution.py:235
  23.2 1.7 %collective-permute-start.18 = (bf16[64,512]{1,0:T(8,128)(2,1)S(1)}, bf16[64,512]{1,0:T(8,128)(2,1)S(1)}, u32[]{:S(2)}, u32[]{:S(2)}) collective-permute-start(bf16[64,512]{1,0:T(8,128)(2,1)S(1)} %bitcast.50), channel_id=1, source_target_pairs={{0,3},{1,2},{2,1},{3,0},{4,7},{5,6},{6,5},{7,4},{8,11},{9,10},{10,... | collective-permute-start | bytes 196616 | tf_op jit(solution)/shard_map/ppermute | solution.py:235
  24.9 2.4 %collective-permute-done.8.refs_2_ = bf16[512,384]{1,0:T(8,128)(2,1)S(1)} collective-permute-done((bf16[512,384]{1,0:T(8,128)(2,1)S(1)}, bf16[512,384]{1,0:T(8,128)(2,1)S(1)}, u32[]{:S(2)}, u32[]{:S(2)}) %collective-permute-start.8) | collective-permute-done | bytes 393248 | tf_op jit(solution)/shard_map/ppermute | solution.py:250
  27.3 0.2 collective-permute-done.18.b3
  27.6 0.6 shard_map.59.refs_0_
  28.1 1.2 %collective-permute-start.19 = (bf16[256,512]{1,0:T(8,128)(2,1)S(1)}, bf16[256,512]{1,0:T(8,128)(2,1)}, u32[]{:S(2)}, u32[]{:S(2)}) collective-permute-start(bf16[256,512]{1,0:T(8,128)(2,1)S(1)} %shard_map.59.refs_0_), channel_id=1, source_target_pairs={{0,8},{1,9},{2,10},{3,11},{8,12},{9,13},{10,14},{11,15},{12,4},{13... | collective-permute-start | bytes 786440 | tf_op jit(solution)/shard_map/ppermute | solution.py:250
  29.3 0.7 slice.71
  30.1 0.7 slice.72
  30.8 3.2 %collective-permute-start.3 = (bf16[64,2048]{1,0:T(8,128)(2,1)}, bf16[64,2048]{1,0:T(8,128)(2,1)}, u32[]{:S(2)}, u32[]{:S(2)}) collective-permute-start(bf16[64,2048]{1,0:T(8,128)(2,1)} %slice.72), channel_id=1, source_target_pairs={{0,1},{1,0},{2,3},{3,2},{4,5},{5,4},{6,7},{7,6},{8,9},{9,8},{10,11... | collective-permute-start | bytes 786440 | tf_op jit(solution)/shard_map/ppermute | solution.py:235
  34.0 1.0 fusion
  35.0 0.1 copy.27.cos_ref
  35.1 0.9 pad_maximum_fusion.1
  36.0 0.7 tile.20
  36.7 1.1 %copy.28.sin_ref = f32[512,128]{1,0:T(8,128)S(1)} copy(f32[512,128]{0,1:T(8,128)} %bitcast.45) | data formatting | bytes 524288 | tf_op jit(solution)/shard_map/tile | solution.py:298
  37.8 0.5 collective-permute-done.3.x3b
  38.3 1.9 %shard_map.55 = (bf16[512,2048]{1,0:T(8,128)(2,1)S(1)}, bf16[512,512]{1,0:T(8,128)(2,1)S(1)}) custom-call(s32[64]{0:T(128)S(1)} %get-tuple-element.69.s_ref, bf16[128,2048]{1,0:T(8,128)(2,1)S(1)} %bitcast.39, bf16[128,2048]{1,0:T(8,128)(2,1)S(1)} %collective-permute-done.x1, bf16[128,2048]{1,0:T(8,128)(2,1)S(1)} %collective-permute-done.1.x2, ...), custom_call_target="tpu_custom_call" | custom-call | bytes 4194304 | tf_op jit(solution)/shard_map/pallas_call | solution.py:26
  40.2 2.6 %shard_map.57 = (bf16[512,256]{1,0:T(8,128)(2,1)S(1)}, bf16[512,128]{1,0:T(8,128)(2,1)S(1)}) custom-call(s32[64]{0:T(128)S(1)} %get-tuple-element.69.s_ref, bf16[512,2048]{1,0:T(8,128)(2,1)S(1)} %get-tuple-element.61.normed_ref, f32[512,128]{1,0:T(8,128)S(1)} %copy.27.cos_ref, f32[512,128]{1,0:T(8,128)S(1)} %copy.28.sin_ref, ...), custom_call_target="tpu_custom_call" | custom-call | flops 805306368 | bytes 3670016 | tf_op jit(solution)/shard_map/pallas_call | solution.py:26
  42.8 1.3 %collective-permute-start.10 = (bf16[512,128]{1,0:T(8,128)(2,1)S(1)}, bf16[512,128]{1,0:T(8,128)(2,1)S(1)}, u32[]{:S(2)}, u32[]{:S(2)}) collective-permute-start(bf16[512,128]{1,0:T(8,128)(2,1)S(1)} %get-tuple-element.63.refs_2_), channel_id=1, source_target_pairs={{0,8},{1,9},{2,10},{3,11},{4,12},{5,13},{6,14},{7,15},{16,24},{17,... | collective-permute-start | bytes 393224 | tf_op jit(solution)/shard_map/ppermute | solution.py:315
  44.1 1.9 %collective-permute-start.11 = (bf16[512,128]{1,0:T(8,128)(2,1)S(1)}, bf16[512,128]{1,0:T(8,128)(2,1)S(1)}, u32[]{:S(2)}, u32[]{:S(2)}) collective-permute-start(bf16[512,128]{1,0:T(8,128)(2,1)S(1)} %get-tuple-element.63.refs_2_), channel_id=1, source_target_pairs={{0,4},{1,5},{2,6},{3,7},{4,8},{5,9},{6,10},{7,11},{8,12},{9,13},{1... | collective-permute-start | bytes 393224 | tf_op jit(solution)/shard_map/ppermute | solution.py:315
  46.1 3.4 %collective-permute-done.10.refs_0_ = bf16[512,128]{1,0:T(8,128)(2,1)S(1)} collective-permute-done((bf16[512,128]{1,0:T(8,128)(2,1)S(1)}, bf16[512,128]{1,0:T(8,128)(2,1)S(1)}, u32[]{:S(2)}, u32[]{:S(2)}) %collective-permute-start.10) | collective-permute-done | bytes 131104 | tf_op jit(solution)/shard_map/ppermute | solution.py:315
  49.5 1.5 %collective-permute-done.11.refs_1_ = bf16[512,128]{1,0:T(8,128)(2,1)S(1)} collective-permute-done((bf16[512,128]{1,0:T(8,128)(2,1)S(1)}, bf16[512,128]{1,0:T(8,128)(2,1)S(1)}, u32[]{:S(2)}, u32[]{:S(2)}) %collective-permute-start.11) | collective-permute-done | bytes 131104 | tf_op jit(solution)/shard_map/ppermute | solution.py:315
  51.1 5.2 %shard_map.58.a0 = bf16[512,256]{1,0:T(8,128)(2,1)S(1)} custom-call(s32[64]{0:T(128)S(1)} %get-tuple-element.69.s_ref, bf16[512,256]{1,0:T(8,128)(2,1)S(1)} %get-tuple-element.62.q_ref, bf16[512,128]{1,0:T(8,128)(2,1)S(1)} %collective-permute-done.10.refs_0_, bf16[512,128]{1,0:T(8,128)(2,1)S(1)} %collective-permute-done.11.refs_1_, ...), custom_call_target="tpu_custom_call" | custom-call | flops 536870912 | bytes 524288 | tf_op jit(solution)/shard_map/pallas_call | solution.py:26
  56.3 1.5 %collective-permute-start.12 = (bf16[512,256]{1,0:T(8,128)(2,1)S(1)}, bf16[512,256]{1,0:T(8,128)(2,1)S(1)}, u32[]{:S(2)}, u32[]{:S(2)}) collective-permute-start(bf16[512,256]{1,0:T(8,128)(2,1)S(1)} %shard_map.58.a0), channel_id=1, source_target_pairs={{0,1},{1,0},{2,3},{3,2},{4,5},{5,4},{6,7},{7,6},{8,9},{9,8},{10,11... | collective-permute-start | bytes 786440 | tf_op jit(solution)/shard_map/ppermute | solution.py:235
  57.8 1.5 %collective-permute-start.13 = (bf16[512,256]{1,0:T(8,128)(2,1)S(1)}, bf16[512,256]{1,0:T(8,128)(2,1)S(1)}, u32[]{:S(2)}, u32[]{:S(2)}) collective-permute-start(bf16[512,256]{1,0:T(8,128)(2,1)S(1)} %shard_map.58.a0), channel_id=1, source_target_pairs={{0,2},{1,3},{2,0},{3,1},{4,6},{5,7},{6,4},{7,5},{8,10},{9,11},{10,... | collective-permute-start | bytes 786440 | tf_op jit(solution)/shard_map/ppermute | solution.py:235
  59.3 2.3 %collective-permute-start.21 = (bf16[256,512]{1,0:T(8,128)(2,1)S(1)}, bf16[256,512]{1,0:T(8,128)(2,1)S(1)}, u32[]{:S(2)}, u32[]{:S(2)}) collective-permute-start(bf16[256,512]{1,0:T(8,128)(2,1)S(1)} %collective-permute-done.20.refs_2_), channel_id=1, source_target_pairs={{0,8},{1,9},{2,10},{3,11},{8,12},{9,13},{10,14},{11,15},{12,4},{13... | collective-permute-start | bytes 786440 | tf_op jit(solution)/shard_map/ppermute | solution.py:250
  61.6 1.5 %collective-permute-start.14 = (bf16[256,256]{1,0:T(8,128)(2,1)S(1)}, bf16[256,256]{1,0:T(8,128)(2,1)S(1)}, u32[]{:S(2)}, u32[]{:S(2)}) collective-permute-start(bf16[256,256]{1,0:T(8,128)(2,1)S(1)} %slice.76), channel_id=1, source_target_pairs={{0,2},{1,3},{2,0},{3,1},{4,6},{5,7},{6,4},{7,5},{8,10},{9,11},{10,... | collective-permute-start | bytes 393224 | tf_op jit(solution)/shard_map/ppermute | solution.py:235
  63.2 1.8 %collective-permute-start.15 = (bf16[256,256]{1,0:T(8,128)(2,1)S(1)}, bf16[256,256]{1,0:T(8,128)(2,1)S(1)}, u32[]{:S(2)}, u32[]{:S(2)}) collective-permute-start(bf16[256,256]{1,0:T(8,128)(2,1)S(1)} %slice.77), channel_id=1, source_target_pairs={{0,1},{1,0},{2,3},{3,2},{4,5},{5,4},{6,7},{7,6},{8,9},{9,8},{10,11... | collective-permute-start | bytes 393224 | tf_op jit(solution)/shard_map/ppermute | solution.py:235
  65.0 0.4 collective-permute-done.21.refs_3_
  65.4 0.1 collective-permute-done.14.a3a
  65.5 1.8 %collective-permute-done.15.a3b = bf16[256,256]{1,0:T(8,128)(2,1)S(1)} collective-permute-done((bf16[256,256]{1,0:T(8,128)(2,1)S(1)}, bf16[256,256]{1,0:T(8,128)(2,1)S(1)}, u32[]{:S(2)}, u32[]{:S(2)}) %collective-permute-start.15) | collective-permute-done | bytes 131104 | tf_op jit(solution)/shard_map/ppermute | solution.py:235
  67.3 1.7 %shard_map.60 = (bf16[128,512]{1,0:T(8,128)(2,1)S(1)}, bf16[128,512]{1,0:T(8,128)(2,1)S(1)}, bf16[128,512]{1,0:T(8,128)(2,1)S(1)}, bf16[128,512]{1,0:T(8,128)(2,1)S(1)}) custom-call(s32[64]{0:T(128)S(1)} %get-tuple-element.69.s_ref, bf16[512,256]{1,0:T(8,128)(2,1)S(1)} %shard_map.58.a0, bf16[512,256]{1,0:T(8,128)(2,1)S(1)} %collective-permute-done.12.a1, ...), custom_call_target="tpu_custom_call" | custom-call | flops 536870912 | bytes 2097152 | tf_op jit(solution)/shard_map/pallas_call | solution.py:26
  69.1 19.6 %collective-permute-start.22 = (bf16[128,512]{1,0:T(8,128)(2,1)S(1)}, bf16[128,512]{1,0:T(8,128)(2,1)S(1)}, u32[]{:S(2)}, u32[]{:S(2)}) collective-permute-start(bf16[128,512]{1,0:T(8,128)(2,1)S(1)} %get-tuple-element.65), channel_id=1, source_target_pairs={{0,16},{1,17},{2,18},{3,19},{4,20},{5,21},{6,22},{7,23},{8,24},{9,... | collective-permute-start | bytes 393224 | tf_op jit(solution)/shard_map/ppermute | solution.py:349
  88.7 1.7 %collective-permute-start.23 = (bf16[128,512]{1,0:T(8,128)(2,1)S(1)}, bf16[128,512]{1,0:T(8,128)(2,1)S(1)}, u32[]{:S(2)}, u32[]{:S(2)}) collective-permute-start(bf16[128,512]{1,0:T(8,128)(2,1)S(1)} %get-tuple-element.66), channel_id=1, source_target_pairs={{0,17},{1,16},{2,19},{3,18},{4,21},{5,20},{6,23},{7,22},{8,25},{9,... | collective-permute-start | bytes 393224 | tf_op jit(solution)/shard_map/ppermute | solution.py:349
  90.4 0.1 collective-permute-start.24
  90.5 1.4 %collective-permute-start.25 = (bf16[128,512]{1,0:T(8,128)(2,1)S(1)}, bf16[128,512]{1,0:T(8,128)(2,1)S(1)}, u32[]{:S(2)}, u32[]{:S(2)}) collective-permute-start(bf16[128,512]{1,0:T(8,128)(2,1)S(1)} %get-tuple-element.68), channel_id=1, source_target_pairs={{0,19},{1,18},{2,17},{3,16},{4,23},{5,22},{6,21},{7,20},{8,27},{9,... | collective-permute-start | bytes 393224 | tf_op jit(solution)/shard_map/ppermute | solution.py:349
  91.9 2.6 %collective-permute-done.23.r1 = bf16[128,512]{1,0:T(8,128)(2,1)S(1)} collective-permute-done((bf16[128,512]{1,0:T(8,128)(2,1)S(1)}, bf16[128,512]{1,0:T(8,128)(2,1)S(1)}, u32[]{:S(2)}, u32[]{:S(2)}) %collective-permute-start.23) | collective-permute-done | bytes 131104 | tf_op jit(solution)/shard_map/ppermute | solution.py:349
  94.5 4.3 %collective-permute-done.24.r2 = bf16[128,512]{1,0:T(8,128)(2,1)S(1)} collective-permute-done((bf16[128,512]{1,0:T(8,128)(2,1)S(1)}, bf16[128,512]{1,0:T(8,128)(2,1)S(1)}, u32[]{:S(2)}, u32[]{:S(2)}) %collective-permute-start.24) | collective-permute-done | bytes 131104 | tf_op jit(solution)/shard_map/ppermute | solution.py:349
  98.8 0.6 shard_map.61
  99.4 0.8 copy.48
  (38 shorter events, 0.3 us)
Async XLA Ops:
  0.0 4.8 %copy-start.3 = (s32[2,4]{1,0:T(2,128)S(1)}, s32[2,4]{1,0:T(2,128)}, u32[]{:S(2)}) copy-start(s32[2,4]{1,0:T(2,128)} %param.17) | copy-start | bytes 100
  1.2 9.6 %copy-start = (bf16[1,128,2048]{2,1,0:T(8,128)(2,1)S(1)}, bf16[1,128,2048]{2,1,0:T(8,128)(2,1)}, u32[]{:S(2)}) copy-start(bf16[1,128,2048]{2,1,0:T(8,128)(2,1)} %param.13) | copy-start | bytes 1572868
  1.2 11.2 %copy-start.2 = (bf16[1,64,2048]{2,1,0:T(8,128)(2,1)S(1)}, bf16[1,64,2048]{2,1,0:T(8,128)(2,1)}, u32[]{:S(2)}) copy-start(bf16[1,64,2048]{2,1,0:T(8,128)(2,1)} %param.16) | copy-start | bytes 786436
  2.0 3.5 %collective-permute-start.4 = (bf16[128,384]{1,0:T(8,128)(2,1)S(1)}, bf16[128,384]{1,0:T(8,128)(2,1)S(1)}, u32[]{:S(2)}, u32[]{:S(2)}) collective-permute-start(bf16[128,384]{1,0:T(8,128)(2,1)S(1)} %get-tuple-element.73), channel_id=1, source_target_pairs={{0,1},{1,0},{2,3},{3,2},{4,5},{5,4},{6,7},{7,6},{8,9},{9,8},{10,11... | collective-permute-start | bytes 294920 | tf_op jit(solution)/shard_map/ppermute | solution.py:235
  3.2 3.7 %collective-permute-start.5 = (bf16[128,384]{1,0:T(8,128)(2,1)S(1)}, bf16[128,384]{1,0:T(8,128)(2,1)S(1)}, u32[]{:S(2)}, u32[]{:S(2)}) collective-permute-start(bf16[128,384]{1,0:T(8,128)(2,1)S(1)} %get-tuple-element.72), channel_id=1, source_target_pairs={{0,2},{1,3},{2,0},{3,1},{4,6},{5,7},{6,4},{7,5},{8,10},{9,11},{10,... | collective-permute-start | bytes 294920 | tf_op jit(solution)/shard_map/ppermute | solution.py:235
  4.5 4.5 %collective-permute-start.6 = (bf16[128,384]{1,0:T(8,128)(2,1)S(1)}, bf16[128,384]{1,0:T(8,128)(2,1)S(1)}, u32[]{:S(2)}, u32[]{:S(2)}) collective-permute-start(bf16[128,384]{1,0:T(8,128)(2,1)S(1)} %get-tuple-element.71), channel_id=1, source_target_pairs={{0,3},{1,2},{2,1},{3,0},{4,7},{5,6},{6,5},{7,4},{8,11},{9,10},{10,... | collective-permute-start | bytes 294920 | tf_op jit(solution)/shard_map/ppermute | solution.py:235
  9.5 9.3 %collective-permute-start.7 = (bf16[512,384]{1,0:T(8,128)(2,1)S(1)}, bf16[512,384]{1,0:T(8,128)(2,1)S(1)}, u32[]{:S(2)}, u32[]{:S(2)}) collective-permute-start(bf16[512,384]{1,0:T(8,128)(2,1)S(1)} %shard_map.56.refs_0_), channel_id=1, source_target_pairs={{0,8},{1,9},{2,10},{3,11},{8,12},{9,13},{10,14},{11,15},{12,4},{13... | collective-permute-start | bytes 1179656 | tf_op jit(solution)/shard_map/ppermute | solution.py:250
  10.9 18.4 %collective-permute-start = (bf16[128,2048]{1,0:T(8,128)(2,1)S(1)}, bf16[128,2048]{1,0:T(8,128)(2,1)S(1)}, u32[]{:S(2)}, u32[]{:S(2)}) collective-permute-start(bf16[128,2048]{1,0:T(8,128)(2,1)S(1)} %bitcast.37), channel_id=1, source_target_pairs={{0,1},{1,0},{2,3},{3,2},{4,5},{5,4},{6,7},{7,6},{8,9},{9,8},{10,11... | collective-permute-start | bytes 1572872 | tf_op jit(solution)/shard_map/ppermute | solution.py:235
  12.2 17.9 %collective-permute-start.1 = (bf16[128,2048]{1,0:T(8,128)(2,1)S(1)}, bf16[128,2048]{1,0:T(8,128)(2,1)S(1)}, u32[]{:S(2)}, u32[]{:S(2)}) collective-permute-start(bf16[128,2048]{1,0:T(8,128)(2,1)S(1)} %bitcast.38), channel_id=1, source_target_pairs={{0,2},{1,3},{2,0},{3,1},{4,6},{5,7},{6,4},{7,5},{8,10},{9,11},{10,... | collective-permute-start | bytes 1572872 | tf_op jit(solution)/shard_map/ppermute | solution.py:235
  13.2 10.1 %collective-permute-start.16 = (bf16[64,512]{1,0:T(8,128)(2,1)S(1)}, bf16[64,512]{1,0:T(8,128)(2,1)S(1)}, u32[]{:S(2)}, u32[]{:S(2)}) collective-permute-start(bf16[64,512]{1,0:T(8,128)(2,1)S(1)} %bitcast.49), channel_id=1, source_target_pairs={{0,1},{1,0},{2,3},{3,2},{4,5},{5,4},{6,7},{7,6},{8,9},{9,8},{10,11... | collective-permute-start | bytes 196616 | tf_op jit(solution)/shard_map/ppermute | solution.py:235
  13.4 13.9 %collective-permute-start.17 = (bf16[64,512]{1,0:T(8,128)(2,1)S(1)}, bf16[64,512]{1,0:T(8,128)(2,1)S(1)}, u32[]{:S(2)}, u32[]{:S(2)}) collective-permute-start(bf16[64,512]{1,0:T(8,128)(2,1)S(1)} %bitcast.48), channel_id=1, source_target_pairs={{0,2},{1,3},{2,0},{3,1},{4,6},{5,7},{6,4},{7,5},{8,10},{9,11},{10,... | collective-permute-start | bytes 196616 | tf_op jit(solution)/shard_map/ppermute | solution.py:235
  18.9 8.4 %collective-permute-start.8 = (bf16[512,384]{1,0:T(8,128)(2,1)S(1)}, bf16[512,384]{1,0:T(8,128)(2,1)S(1)}, u32[]{:S(2)}, u32[]{:S(2)}) collective-permute-start(bf16[512,384]{1,0:T(8,128)(2,1)S(1)} %collective-permute-done.7.refs_1_), channel_id=1, source_target_pairs={{0,8},{1,9},{2,10},{3,11},{8,12},{9,13},{10,14},{11,15},{12,4},{13... | collective-permute-start | bytes 1179656 | tf_op jit(solution)/shard_map/ppermute | solution.py:250
  19.5 18.8 %copy-start.1 = (f32[1,2048]{1,0:T(1,128)S(1)}, f32[1,2048]{1,0:T(1,128)}, u32[]{:S(2)}) copy-start(f32[1,2048]{1,0:T(1,128)} %gain_ref.1) | copy-start | bytes 24580
  23.2 4.3 %collective-permute-start.18 = (bf16[64,512]{1,0:T(8,128)(2,1)S(1)}, bf16[64,512]{1,0:T(8,128)(2,1)S(1)}, u32[]{:S(2)}, u32[]{:S(2)}) collective-permute-start(bf16[64,512]{1,0:T(8,128)(2,1)S(1)} %bitcast.50), channel_id=1, source_target_pairs={{0,3},{1,2},{2,1},{3,0},{4,7},{5,6},{6,5},{7,4},{8,11},{9,10},{10,... | collective-permute-start | bytes 196616 | tf_op jit(solution)/shard_map/ppermute | solution.py:235
  27.3 12.9 %collective-permute-start.9 = (bf16[512,384]{1,0:T(8,128)(2,1)S(1)}, bf16[512,384]{1,0:T(8,128)(2,1)}, u32[]{:S(2)}, u32[]{:S(2)}) collective-permute-start(bf16[512,384]{1,0:T(8,128)(2,1)S(1)} %collective-permute-done.8.refs_2_), channel_id=1, source_target_pairs={{0,8},{1,9},{2,10},{3,11},{8,12},{9,13},{10,14},{11,15},{12,4},{13... | collective-permute-start | bytes 1179656 | tf_op jit(solution)/shard_map/ppermute | solution.py:250
  28.1 17.9 %collective-permute-start.19 = (bf16[256,512]{1,0:T(8,128)(2,1)S(1)}, bf16[256,512]{1,0:T(8,128)(2,1)}, u32[]{:S(2)}, u32[]{:S(2)}) collective-permute-start(bf16[256,512]{1,0:T(8,128)(2,1)S(1)} %shard_map.59.refs_0_), channel_id=1, source_target_pairs={{0,8},{1,9},{2,10},{3,11},{8,12},{9,13},{10,14},{11,15},{12,4},{13... | collective-permute-start | bytes 786440 | tf_op jit(solution)/shard_map/ppermute | solution.py:250
  30.0 7.7 %collective-permute-start.2 = (bf16[64,2048]{1,0:T(8,128)(2,1)}, bf16[64,2048]{1,0:T(8,128)(2,1)}, u32[]{:S(2)}, u32[]{:S(2)}) collective-permute-start(bf16[64,2048]{1,0:T(8,128)(2,1)} %slice.71), channel_id=1, source_target_pairs={{0,2},{1,3},{2,0},{3,1},{4,6},{5,7},{6,4},{7,5},{8,10},{9,11},{10,... | collective-permute-start | bytes 786440 | tf_op jit(solution)/shard_map/ppermute | solution.py:235
  30.8 7.6 %collective-permute-start.3 = (bf16[64,2048]{1,0:T(8,128)(2,1)}, bf16[64,2048]{1,0:T(8,128)(2,1)}, u32[]{:S(2)}, u32[]{:S(2)}) collective-permute-start(bf16[64,2048]{1,0:T(8,128)(2,1)} %slice.72), channel_id=1, source_target_pairs={{0,1},{1,0},{2,3},{3,2},{4,5},{5,4},{6,7},{7,6},{8,9},{9,8},{10,11... | collective-permute-start | bytes 786440 | tf_op jit(solution)/shard_map/ppermute | solution.py:235
  42.8 6.7 %collective-permute-start.10 = (bf16[512,128]{1,0:T(8,128)(2,1)S(1)}, bf16[512,128]{1,0:T(8,128)(2,1)S(1)}, u32[]{:S(2)}, u32[]{:S(2)}) collective-permute-start(bf16[512,128]{1,0:T(8,128)(2,1)S(1)} %get-tuple-element.63.refs_2_), channel_id=1, source_target_pairs={{0,8},{1,9},{2,10},{3,11},{4,12},{5,13},{6,14},{7,15},{16,24},{17,... | collective-permute-start | bytes 393224 | tf_op jit(solution)/shard_map/ppermute | solution.py:315
  44.1 7.0 %collective-permute-start.11 = (bf16[512,128]{1,0:T(8,128)(2,1)S(1)}, bf16[512,128]{1,0:T(8,128)(2,1)S(1)}, u32[]{:S(2)}, u32[]{:S(2)}) collective-permute-start(bf16[512,128]{1,0:T(8,128)(2,1)S(1)} %get-tuple-element.63.refs_2_), channel_id=1, source_target_pairs={{0,4},{1,5},{2,6},{3,7},{4,8},{5,9},{6,10},{7,11},{8,12},{9,13},{1... | collective-permute-start | bytes 393224 | tf_op jit(solution)/shard_map/ppermute | solution.py:315
  46.1 13.2 %collective-permute-start.20 = (bf16[256,512]{1,0:T(8,128)(2,1)}, bf16[256,512]{1,0:T(8,128)(2,1)S(1)}, u32[]{:S(2)}, u32[]{:S(2)}) collective-permute-start(bf16[256,512]{1,0:T(8,128)(2,1)} %collective-permute-done.19.refs_1_), channel_id=1, source_target_pairs={{0,8},{1,9},{2,10},{3,11},{8,12},{9,13},{10,14},{11,15},{12,4},{13... | collective-permute-start | bytes 786440 | tf_op jit(solution)/shard_map/ppermute | solution.py:250
  56.3 5.3 %collective-permute-start.12 = (bf16[512,256]{1,0:T(8,128)(2,1)S(1)}, bf16[512,256]{1,0:T(8,128)(2,1)S(1)}, u32[]{:S(2)}, u32[]{:S(2)}) collective-permute-start(bf16[512,256]{1,0:T(8,128)(2,1)S(1)} %shard_map.58.a0), channel_id=1, source_target_pairs={{0,1},{1,0},{2,3},{3,2},{4,5},{5,4},{6,7},{7,6},{8,9},{9,8},{10,11... | collective-permute-start | bytes 786440 | tf_op jit(solution)/shard_map/ppermute | solution.py:235
  57.8 5.3 %collective-permute-start.13 = (bf16[512,256]{1,0:T(8,128)(2,1)S(1)}, bf16[512,256]{1,0:T(8,128)(2,1)S(1)}, u32[]{:S(2)}, u32[]{:S(2)}) collective-permute-start(bf16[512,256]{1,0:T(8,128)(2,1)S(1)} %shard_map.58.a0), channel_id=1, source_target_pairs={{0,2},{1,3},{2,0},{3,1},{4,6},{5,7},{6,4},{7,5},{8,10},{9,11},{10,... | collective-permute-start | bytes 786440 | tf_op jit(solution)/shard_map/ppermute | solution.py:235
  59.3 6.1 %collective-permute-start.21 = (bf16[256,512]{1,0:T(8,128)(2,1)S(1)}, bf16[256,512]{1,0:T(8,128)(2,1)S(1)}, u32[]{:S(2)}, u32[]{:S(2)}) collective-permute-start(bf16[256,512]{1,0:T(8,128)(2,1)S(1)} %collective-permute-done.20.refs_2_), channel_id=1, source_target_pairs={{0,8},{1,9},{2,10},{3,11},{8,12},{9,13},{10,14},{11,15},{12,4},{13... | collective-permute-start | bytes 786440 | tf_op jit(solution)/shard_map/ppermute | solution.py:250
  61.6 3.9 %collective-permute-start.14 = (bf16[256,256]{1,0:T(8,128)(2,1)S(1)}, bf16[256,256]{1,0:T(8,128)(2,1)S(1)}, u32[]{:S(2)}, u32[]{:S(2)}) collective-permute-start(bf16[256,256]{1,0:T(8,128)(2,1)S(1)} %slice.76), channel_id=1, source_target_pairs={{0,2},{1,3},{2,0},{3,1},{4,6},{5,7},{6,4},{7,5},{8,10},{9,11},{10,... | collective-permute-start | bytes 393224 | tf_op jit(solution)/shard_map/ppermute | solution.py:235
  63.2 4.2 %collective-permute-start.15 = (bf16[256,256]{1,0:T(8,128)(2,1)S(1)}, bf16[256,256]{1,0:T(8,128)(2,1)S(1)}, u32[]{:S(2)}, u32[]{:S(2)}) collective-permute-start(bf16[256,256]{1,0:T(8,128)(2,1)S(1)} %slice.77), channel_id=1, source_target_pairs={{0,1},{1,0},{2,3},{3,2},{4,5},{5,4},{6,7},{7,6},{8,9},{9,8},{10,11... | collective-permute-start | bytes 393224 | tf_op jit(solution)/shard_map/ppermute | solution.py:235
  69.1 22.9 %collective-permute-start.22 = (bf16[128,512]{1,0:T(8,128)(2,1)S(1)}, bf16[128,512]{1,0:T(8,128)(2,1)S(1)}, u32[]{:S(2)}, u32[]{:S(2)}) collective-permute-start(bf16[128,512]{1,0:T(8,128)(2,1)S(1)} %get-tuple-element.65), channel_id=1, source_target_pairs={{0,16},{1,17},{2,18},{3,19},{4,20},{5,21},{6,22},{7,23},{8,24},{9,... | collective-permute-start | bytes 393224 | tf_op jit(solution)/shard_map/ppermute | solution.py:349
  88.7 5.8 %collective-permute-start.23 = (bf16[128,512]{1,0:T(8,128)(2,1)S(1)}, bf16[128,512]{1,0:T(8,128)(2,1)S(1)}, u32[]{:S(2)}, u32[]{:S(2)}) collective-permute-start(bf16[128,512]{1,0:T(8,128)(2,1)S(1)} %get-tuple-element.66), channel_id=1, source_target_pairs={{0,17},{1,16},{2,19},{3,18},{4,21},{5,20},{6,23},{7,22},{8,25},{9,... | collective-permute-start | bytes 393224 | tf_op jit(solution)/shard_map/ppermute | solution.py:349
  90.4 8.4 %collective-permute-start.24 = (bf16[128,512]{1,0:T(8,128)(2,1)S(1)}, bf16[128,512]{1,0:T(8,128)(2,1)S(1)}, u32[]{:S(2)}, u32[]{:S(2)}) collective-permute-start(bf16[128,512]{1,0:T(8,128)(2,1)S(1)} %get-tuple-element.67), channel_id=1, source_target_pairs={{0,18},{1,19},{2,16},{3,17},{4,22},{5,23},{6,20},{7,21},{8,26},{9,... | collective-permute-start | bytes 393224 | tf_op jit(solution)/shard_map/ppermute | solution.py:349
  90.5 8.3 %collective-permute-start.25 = (bf16[128,512]{1,0:T(8,128)(2,1)S(1)}, bf16[128,512]{1,0:T(8,128)(2,1)S(1)}, u32[]{:S(2)}, u32[]{:S(2)}) collective-permute-start(bf16[128,512]{1,0:T(8,128)(2,1)S(1)} %get-tuple-element.68), channel_id=1, source_target_pairs={{0,19},{1,18},{2,17},{3,16},{4,23},{5,22},{6,21},{7,20},{8,27},{9,... | collective-permute-start | bytes 393224 | tf_op jit(solution)/shard_map/ppermute | solution.py:349
